TPU v7x, 512 devices: a whole 4x8x8 slice. The times are simulated.
512 devices in a mesh: gx: 32 (over x, y), gy: 8 (over z_lo, core), gz: 2 (over z_hi).
Axes of the slice: x: 4, y: 8, z: 8 (z_hi: 2, z_lo: 4; z = z_hi * 4 + z_lo), core: 2. Of those that a mesh axis runs over, the one named last changes fastest.
Arguments:
- populations: float32 [19, 128, 32, 2048], P(None, 'gx', 'gz', 'gy'), may hold values from 0.01 to 0.21
- nozzle_mask: int32 [128, 2048], P('gx', 'gy'), may hold values 0 or 1
- wall_type: int32 [128, 2048], P('gx', 'gy'), may hold values from 0 to 1
- solid_temp: float32 [128, 64, 2048], P('gx', None, ('gy', 'gz')), may hold values from -6 to 6
- diffusion: float32 [128, 64, 2048], P('gx', None, ('gy', 'gz')), may hold values from 0.3 to 3
- heat_load: float32 [128, 2048], P('gx', ('gy', 'gz')), may hold values from 0.2 to 2
- coolant_temp: float32 [128, 2048], P('gx', ('gy', 'gz')), may hold values from -2 to 0
Outputs:
- populations_next: float32 [19, 128, 32, 2048], P(None, 'gx', 'gz', 'gy')
- solid_next: float32 [128, 64, 2048], P('gx', None, ('gy', 'gz'))
Inputs may be any that keep to these rules, and one draw needn't show every extreme that they name: `nozzle_mask`: 1 marks a nozzle opening; it takes precedence over wall_type. `wall_type`: 1 marks an outlet cell of the plate, 0 a closed plate cell.
All inputs are finite; a program needn't handle non-finite values. No bound on the sum of `nozzle_mask` on one device may be relied on, other than what follows from the above.
Results may differ from a plain program's by a relative error of at most 0.0001.
Values sent between devices are 32-bit elements; how exact they have to be, the bound alone decides.
No kernel may reach another device: no remote copies, remote signals or barrier semaphores. Data moves between devices by JAX's collectives and lax.ppermute only.
A program may use at most 64 MiB of HBM per device.

v0:
```python
import jax
import jax.numpy as jnp
import numpy as np
from jax import lax
from jax.sharding import PartitionSpec as P

JET_SPEED = 0.1
H_BASE = 0.5
H_GAIN = 40.0
SHEAR_RATE = 1.6
ODD_RATE = 1.2
EVEN_RATE = 1.4


def broadcast(block, axis, holder):
    block = jnp.where(lax.axis_index(axis) == holder, block, jnp.zeros_like(block))
    return lax.psum(block, axis)


def padded_2(block, sides, width):
    for axis, dim in sides:
        count = lax.axis_size(axis)
        forward = [(i, i + 1) for i in range(count - 1)]
        forward.append((count - 1, 0))
        backward = [(target, source) for source, target in forward]
        low = lax.ppermute(
            lax.slice_in_dim(block, block.shape[dim] - width, None, axis=dim), axis, forward
        )
        high = lax.ppermute(lax.slice_in_dim(block, 0, width, axis=dim), axis, backward)
        block = jnp.concatenate([low, block, high], axis=dim)
    return block


def velocity_table():
    return np.array(
        [
            [0, 0, 0],
            [1, 0, 0],
            [-1, 0, 0],
            [0, 1, 0],
            [0, -1, 0],
            [0, 0, 1],
            [0, 0, -1],
            [1, 1, 0],
            [-1, -1, 0],
            [1, -1, 0],
            [-1, 1, 0],
            [1, 0, 1],
            [-1, 0, -1],
            [1, 0, -1],
            [-1, 0, 1],
            [0, 1, 1],
            [0, -1, -1],
            [0, 1, -1],
            [0, -1, 1],
        ],
        dtype=np.int32,
    )


def weight_table():
    return np.array([1.0 / 3.0] + [1.0 / 18.0] * 6 + [1.0 / 36.0] * 12, dtype=np.float32)


def opposite_of(member):
    table = velocity_table()
    for other in range(table.shape[0]):
        if np.all(table[other] == -table[member]):
            return other
    return member


def relax_table():
    table = velocity_table().astype(np.float32)
    comp_a = table[:, 0]
    comp_b = table[:, 1]
    comp_c = table[:, 2]
    monomials = [
        comp_a * 0.0 + 1.0,
        comp_a,
        comp_b,
        comp_c,
        comp_a * comp_a,
        comp_b * comp_b,
        comp_c * comp_c,
        comp_a * comp_b,
        comp_b * comp_c,
        comp_a * comp_c,
        comp_a * comp_c * comp_c,
        comp_a * comp_b * comp_b,
        comp_c * comp_a * comp_a,
        comp_c * comp_b * comp_b,
        comp_b * comp_a * comp_a,
        comp_b * comp_c * comp_c,
        comp_a * comp_a * comp_c * comp_c,
        comp_a * comp_a * comp_b * comp_b,
        comp_c * comp_c * comp_b * comp_b,
    ]
    rates = np.array(
        [0.0] * 4 + [SHEAR_RATE] * 6 + [ODD_RATE] * 6 + [EVEN_RATE] * 3, dtype=np.float32
    )
    ortho = []
    for monomial in monomials:
        vector = monomial.copy()
        for earlier in ortho:
            vector = vector - np.dot(earlier, vector) * earlier
        ortho.append(vector / np.sqrt(np.dot(vector, vector)))
    gram = np.stack(ortho)
    return (gram.T @ (rates[:, None] * gram)).astype(np.float32)


def collide(pops):
    table = jnp.asarray(velocity_table().astype(np.float32))
    weights = jnp.asarray(weight_table())
    density = jnp.sum(pops, axis=0)
    momentum = jnp.einsum("qc,qxzy->cxzy", table, pops, precision=lax.Precision.HIGHEST)
    velocity = momentum / density[None]
    project = jnp.einsum("qc,cxzy->qxzy", table, velocity, precision=lax.Precision.HIGHEST)
    square = jnp.sum(velocity * velocity, axis=0)
    equil = (
        weights[:, None, None, None]
        * density[None]
        * (1.0 + 3.0 * project + 4.5 * project * project - 1.5 * square[None])
    )
    relaxed = jnp.einsum(
        "pq,qxzy->pxzy", jnp.asarray(relax_table()), pops - equil, precision=lax.Precision.HIGHEST
    )
    return (pops - relaxed, density, velocity)


def wall_coefficient(velocity_plane):
    return H_BASE + H_GAIN * jnp.sum(velocity_plane * velocity_plane, axis=0)


def apply_walls(moved, post, nozzle, outlet_kind, at_bottom, at_top):
    table = velocity_table()
    weights = weight_table()
    layers = []
    for member in range(table.shape[0]):
        layer = moved[member]
        other = opposite_of(member)
        if table[member, 2] > 0:
            bottom_value = post[other][:, 0, :]
            layer = layer.at[:, 0, :].set(jnp.where(at_bottom, bottom_value, layer[:, 0, :]))
        if table[member, 2] < 0:
            closed_value = post[other][:, -1, :]
            inlet_value = closed_value + 6.0 * float(weights[member]) * JET_SPEED
            outlet_value = post[member][:, -1, :]
            top_value = jnp.where(
                nozzle == 1, inlet_value, jnp.where(outlet_kind == 1, outlet_value, closed_value)
            )
            layer = layer.at[:, -1, :].set(jnp.where(at_top, top_value, layer[:, -1, :]))
        layers.append(layer)
    return jnp.stack(layers)


def sweep_core(temp, cond, told, load, heat, coolant, neighbours):
    numer = told
    denom = jnp.ones_like(told)
    for near_temp, near_cond in neighbours:
        link = 0.5 * (cond + near_cond)
        numer = numer + link * near_temp
        denom = denom + link
    link = 0.5 * (cond[:, 1:] + cond[:, :-1])
    edge = jnp.zeros_like(cond[:, :1])
    numer = numer + jnp.concatenate([link * temp[:, 1:], edge], axis=1)
    denom = denom + jnp.concatenate([link, edge], axis=1)
    numer = numer + jnp.concatenate([edge, link * temp[:, :-1]], axis=1)
    denom = denom + jnp.concatenate([edge, link], axis=1)
    numer = numer.at[:, 0].add(load)
    numer = numer.at[:, -1].add(heat * coolant)
    denom = denom.at[:, -1].add(heat)
    return numer / denom


def cycle_of(temp, cond):
    return [
        (temp[:-2, :, 1:-1], cond[:-2, :, 1:-1]),
        (temp[2:, :, 1:-1], cond[2:, :, 1:-1]),
        (temp[1:-1, :, :-2], cond[1:-1, :, :-2]),
        (temp[1:-1, :, 2:], cond[1:-1, :, 2:]),
    ]


def body(populations, nozzle_mask, wall_type, solid_temp, diffusion, heat_load, coolant_temp):
    table = velocity_table()
    count = table.shape[0]
    post, density, velocity = collide(populations)
    heat_local = wall_coefficient(velocity[:, :, 0, :])
    tile_width = heat_load.shape[1]
    full_plane = broadcast(heat_local, "gz", 0)
    heat = lax.dynamic_slice_in_dim(full_plane, lax.axis_index("gz") * tile_width, tile_width, 1)
    padded = padded_2(post, (("gx", 1), ("gy", 3), ("gz", 2)), 1)
    span_x, span_z, span_y = (post.shape[1], post.shape[2], post.shape[3])
    moved_list = []
    for member in range(count):
        start_x = 1 - int(table[member, 0])
        start_z = 1 - int(table[member, 2])
        start_y = 1 - int(table[member, 1])
        moved_list.append(
            padded[
                member,
                start_x : start_x + span_x,
                start_z : start_z + span_z,
                start_y : start_y + span_y,
            ]
        )
    moved = jnp.stack(moved_list)
    at_bottom = lax.axis_index("gz") == 0
    at_top = lax.axis_index("gz") == lax.axis_size("gz") - 1
    populations_next = apply_walls(moved, post, nozzle_mask, wall_type, at_bottom, at_top)
    temp_ext, cond_ext = (
        padded_2(solid_temp, (("gx", 0), (("gy", "gz"), 2)), 1),
        padded_2(diffusion, (("gx", 0), (("gy", "gz"), 2)), 1),
    )
    first = sweep_core(
        solid_temp,
        diffusion,
        solid_temp,
        heat_load,
        heat,
        coolant_temp,
        cycle_of(temp_ext, cond_ext),
    )
    first_ext = padded_2(first, (("gx", 0), (("gy", "gz"), 2)), 1)
    solid_next = sweep_core(
        first, diffusion, solid_temp, heat_load, heat, coolant_temp, cycle_of(first_ext, cond_ext)
    )
    return (populations_next, solid_next)


def solution(mesh):
    placed = (
        P(None, "gx", "gz", "gy"),
        P("gx", "gy"),
        P("gx", "gy"),
        P("gx", None, ("gy", "gz")),
        P("gx", None, ("gy", "gz")),
        P("gx", ("gy", "gz")),
        P("gx", ("gy", "gz")),
    )
    return jax.shard_map(
        body,
        mesh=mesh,
        in_specs=placed,
        out_specs=(P(None, "gx", "gz", "gy"), P("gx", None, ("gy", "gz"))),
        check_vma=False,
    )
```

profile of v0, /device:TPU:192, one launch (start us, length us, event | category | flops | bytes accessed | tf_op | source)
XLA Modules:
  0.0 202.7 jit_solution(924696460435875015)
XLA Ops:
  0.7 1.5 fusion.94
  2.1 7.6 %collective-permute-start.9 = (f32[1,64,128]{2,1,0:T(8,128)}, f32[1,64,128]{2,1,0:T(8,128)S(1)}, u32[]{:S(2)}, u32[]{:S(2)}) collective-permute-start(f32[1,64,128]{2,1,0:T(8,128)} %get-tuple-element.243), channel_id=1, source_target_pairs={{16,0},{32,16},{48,32},{64,48},{80,64},{96,80},{112,96},{128,112},... | collective-permute-start | bytes 98312 | tf_op jit(solution)/shard_map/ppermute | solution.py:29
  9.7 1.9 collective-permute-start.7
  13.0 7.2 %collective-permute-start.8 = (f32[1,64,128]{2,1,0:T(8,128)}, f32[1,64,128]{2,1,0:T(8,128)S(1)}, u32[]{:S(2)}, u32[]{:S(2)}) collective-permute-start(f32[1,64,128]{2,1,0:T(8,128)} %get-tuple-element.245), channel_id=1, source_target_pairs={{16,0},{32,16},{48,32},{64,48},{80,64},{96,80},{112,96},{128,112},... | collective-permute-start | bytes 98312 | tf_op jit(solution)/shard_map/ppermute | solution.py:29
  20.3 1.9 collective-permute-start.6
  23.6 1.7 multiply_reduce_fusion
  25.4 1.5 fusion.96
  26.9 2.3 %fusion.2 = f32[19,4,16,256]{3,0,2,1:T(8,128)S(1)} fusion(f32[19,19,1,1]{1,0,3,2:T(8,128)S(1)} %copy-done.27, f32[19,4,16,256]{3,2,1,0:T(8,128)S(1)} %copy-done.1, f32[19,4,16,256]{3,0,2,1:T(8,128)S(1)} %fusion.96, f32[4,16,256]{2,1,0:T(8,128)S(1)} %broadcast_multiply_fusion, f32[4,16,256]{2,1,0:T(8,128)S(1)} %reduce_sum.27, f32[19]{0:T(128)S(1)} %copy-done.33), kind=kOutput, calls=%fused_computation.5 | convolution fusion | flops 73777152 | bytes 3868144 | tf_op jit(solution)/shard_map/pq,qxzy->pxzy/dot_general | solution.py:125
  30.8 1.9 collective-permute-start
  32.8 9.2 %psum.7 = f32[4,256]{1,0:T(4,128)S(1)} all-reduce(f32[4,256]{1,0:T(4,128)S(1)} %add_select_fusion), channel_id=1, replica_groups=mesh['gx'=32,'gy'=8,'gz'=2] {'gz'}, use_global_device_ids=true, to_apply=%region_3.4 | all-reduce | flops 1024 | bytes 8192 | tf_op jit(solution)/shard_map/psum | solution.py:17
  43.1 7.2 %collective-permute-start.1 = (f32[19,1,16,256]{3,1,2,0:T(1,128)}, f32[19,1,16,256]{3,1,2,0:T(1,128)S(1)}, u32[]{:S(2)}, u32[]{:S(2)}) collective-permute-start(f32[19,1,16,256]{3,1,2,0:T(1,128)} %copy.99), channel_id=1, source_target_pairs={{16,0},{32,16},{48,32},{64,48},{80,64},{96,80},{112,96},{128,112},... | collective-permute-start | bytes 933896 | tf_op jit(solution)/shard_map/ppermute | solution.py:29
  51.3 3.9 %collective-permute-start.12 = (f32[6,64,1]{2,1,0:T(8,128)S(1)}, f32[6,64,1]{2,1,0:T(8,128)S(1)}, u32[]{:S(2)}, u32[]{:S(2)}) collective-permute-start(f32[6,64,1]{2,1,0:T(8,128)S(1)} %get-tuple-element.239), channel_id=1, source_target_pairs={{1,0},{2,1},{3,2},{4,3},{5,4},{6,5},{7,6},{8,7},{9,8},{10,9},{11,1... | collective-permute-start | bytes 4616 | tf_op jit(solution)/shard_map/ppermute | solution.py:29
  55.2 5.9 %collective-permute-start.10 = (f32[6,64,1]{2,1,0:T(8,128)S(1)}, f32[6,64,1]{2,1,0:T(8,128)S(1)}, u32[]{:S(2)}, u32[]{:S(2)}) collective-permute-start(f32[6,64,1]{2,1,0:T(8,128)S(1)} %get-tuple-element.240), channel_id=1, source_target_pairs={{0,1},{1,2},{2,3},{3,4},{4,5},{5,6},{6,7},{7,8},{8,9},{9,10},{10,1... | collective-permute-start | bytes 4616 | tf_op jit(solution)/shard_map/ppermute | solution.py:26
  61.2 7.5 %collective-permute-start.11 = (f32[6,64,1]{2,1,0:T(8,128)S(1)}, f32[6,64,1]{2,1,0:T(8,128)S(1)}, u32[]{:S(2)}, u32[]{:S(2)}) collective-permute-start(f32[6,64,1]{2,1,0:T(8,128)S(1)} %get-tuple-element.237), channel_id=1, source_target_pairs={{0,1},{1,2},{2,3},{3,4},{4,5},{5,6},{6,7},{7,8},{8,9},{9,10},{10,1... | collective-permute-start | bytes 4616 | tf_op jit(solution)/shard_map/ppermute | solution.py:26
  68.8 23.2 %collective-permute-done.12 = f32[6,64,1]{2,1,0:T(8,128)S(1)} collective-permute-done((f32[6,64,1]{2,1,0:T(8,128)S(1)}, f32[6,64,1]{2,1,0:T(8,128)S(1)}, u32[]{:S(2)}, u32[]{:S(2)}) %collective-permute-start.12) | collective-permute-done | bytes 1568 | tf_op jit(solution)/shard_map/ppermute | solution.py:29
  92.0 6.9 %collective-permute-start.13 = (f32[6,64,1]{2,1,0:T(8,128)S(1)}, f32[6,64,1]{2,1,0:T(8,128)S(1)}, u32[]{:S(2)}, u32[]{:S(2)}) collective-permute-start(f32[6,64,1]{2,1,0:T(8,128)S(1)} %get-tuple-element.238), channel_id=1, source_target_pairs={{1,0},{2,1},{3,2},{4,3},{5,4},{6,5},{7,6},{8,7},{9,8},{10,9},{11,1... | collective-permute-start | bytes 4616 | tf_op jit(solution)/shard_map/ppermute | solution.py:29
  99.2 4.4 %collective-permute-done.13 = f32[6,64,1]{2,1,0:T(8,128)S(1)} collective-permute-done((f32[6,64,1]{2,1,0:T(8,128)S(1)}, f32[6,64,1]{2,1,0:T(8,128)S(1)}, u32[]{:S(2)}, u32[]{:S(2)}) %collective-permute-start.13) | collective-permute-done | bytes 1568 | tf_op jit(solution)/shard_map/ppermute | solution.py:29
  105.4 1.9 collective-permute-start.14
  107.3 7.2 %collective-permute-start.15 = (f32[1,64,128]{2,1,0:T(8,128)}, f32[1,64,128]{2,1,0:T(8,128)}, u32[]{:S(2)}, u32[]{:S(2)}) collective-permute-start(f32[1,64,128]{2,1,0:T(8,128)} %get-tuple-element.242), channel_id=1, source_target_pairs={{16,0},{32,16},{48,32},{64,48},{80,64},{96,80},{112,96},{128,112},... | collective-permute-start | bytes 98312 | tf_op jit(solution)/shard_map/ppermute | solution.py:29
  117.3 1.9 collective-permute-start.16
  119.3 6.8 %collective-permute-start.17 = (f32[6,64,1]{2,1,0:T(8,128)S(1)}, f32[6,64,1]{2,1,0:T(8,128)S(1)}, u32[]{:S(2)}, u32[]{:S(2)}) collective-permute-start(f32[6,64,1]{2,1,0:T(8,128)S(1)} %get-tuple-element.236), channel_id=1, source_target_pairs={{1,0},{2,1},{3,2},{4,3},{5,4},{6,5},{7,6},{8,7},{9,8},{10,9},{11,1... | collective-permute-start | bytes 4616 | tf_op jit(solution)/shard_map/ppermute | solution.py:29
  127.3 3.4 %collective-permute-done.17 = f32[6,64,1]{2,1,0:T(8,128)S(1)} collective-permute-done((f32[6,64,1]{2,1,0:T(8,128)S(1)}, f32[6,64,1]{2,1,0:T(8,128)S(1)}, u32[]{:S(2)}, u32[]{:S(2)}) %collective-permute-start.17) | collective-permute-done | bytes 1568 | tf_op jit(solution)/shard_map/ppermute | solution.py:29
  135.8 1.6 div.17
  138.3 1.9 fusion.88
  140.1 2.0 copy.104
  142.1 2.0 copy.102
  144.1 1.9 collective-permute-start.2
  146.0 4.7 %collective-permute-start.3 = (f32[19,6,16,1]{0,2,3,1:T(8,128)S(1)}, f32[19,6,16,1]{0,2,3,1:T(8,128)S(1)}, u32[]{:S(2)}, u32[]{:S(2)}) collective-permute-start(f32[19,6,16,1]{0,2,3,1:T(8,128)S(1)} %copy.104), channel_id=1, source_target_pairs={{2,0},{4,2},{6,4},{8,6},{10,8},{12,10},{14,12},{0,14},{3,1},{5,3},... | collective-permute-start | bytes 21896 | tf_op jit(solution)/shard_map/ppermute | solution.py:29
  152.5 2.3 %copy.105 = f32[19,6,16,1]{3,1,2,0:T(8,128)} copy(f32[19,6,16,1]{0,2,3,1:T(8,128)S(1)} %collective-permute-done.3) | data formatting | bytes 14592 | tf_op jit(solution)/shard_map/ppermute | solution.py:29
  157.6 4.8 %collective-permute-start.5 = (f32[19,6,1,258]{3,1,2,0:T(8,128)S(1)}, f32[19,6,1,258]{3,1,2,0:T(8,128)S(1)}, u32[]{:S(2)}, u32[]{:S(2)}) collective-permute-start(f32[19,6,1,258]{3,1,2,0:T(8,128)S(1)} %get-tuple-element.210), channel_id=1, source_target_pairs={{1,0},{0,1},{3,2},{2,3},{5,4},{4,5},{7,6},{6,7},{9,8},{8,9},{11,10... | collective-permute-start | bytes 352952 | tf_op jit(solution)/shard_map/ppermute | solution.py:29
  162.5 5.1 %collective-permute-start.4 = (f32[19,6,1,258]{3,1,2,0:T(8,128)S(1)}, f32[19,6,1,258]{3,1,2,0:T(8,128)S(1)}, u32[]{:S(2)}, u32[]{:S(2)}) collective-permute-start(f32[19,6,1,258]{3,1,2,0:T(8,128)S(1)} %get-tuple-element.211), channel_id=1, source_target_pairs={{0,1},{1,0},{2,3},{3,2},{4,5},{5,4},{6,7},{7,6},{8,9},{9,8},{10,11... | collective-permute-start | bytes 352952 | tf_op jit(solution)/shard_map/ppermute | solution.py:26
  170.8 10.2 %collective-permute-done.5 = f32[19,6,1,258]{3,1,2,0:T(8,128)S(1)} collective-permute-done((f32[19,6,1,258]{3,1,2,0:T(8,128)S(1)}, f32[19,6,1,258]{3,1,2,0:T(8,128)S(1)}, u32[]{:S(2)}, u32[]{:S(2)}) %collective-permute-start.5) | collective-permute-done | bytes 117680 | tf_op jit(solution)/shard_map/ppermute | solution.py:29
  (168 shorter events, 47.7 us)
Async XLA Ops:
  0.6 23.0 %copy-start.32 = (f32[19,3,1,1]{0,1,3,2:T(4,128)S(1)}, f32[19,3,1,1]{0,1,3,2:T(4,128)}, u32[]{:S(2)}) copy-start(f32[19,3,1,1]{0,1,3,2:T(4,128)} %constant.423) | copy-start | bytes 688
  0.6 23.0 %copy-start.1 = (f32[19,4,16,256]{3,2,1,0:T(8,128)S(1)}, f32[19,4,16,256]{3,2,1,0:T(8,128)}, u32[]{:S(2)}) copy-start(f32[19,4,16,256]{3,2,1,0:T(8,128)} %param.42) | copy-start | bytes 3735556
  2.1 59.0 %collective-permute-start.9 = (f32[1,64,128]{2,1,0:T(8,128)}, f32[1,64,128]{2,1,0:T(8,128)S(1)}, u32[]{:S(2)}, u32[]{:S(2)}) collective-permute-start(f32[1,64,128]{2,1,0:T(8,128)} %get-tuple-element.243), channel_id=1, source_target_pairs={{16,0},{32,16},{48,32},{64,48},{80,64},{96,80},{112,96},{128,112},... | collective-permute-start | bytes 98312 | tf_op jit(solution)/shard_map/ppermute | solution.py:29
  9.7 40.8 %collective-permute-start.7 = (f32[1,64,128]{2,1,0:T(8,128)}, f32[1,64,128]{2,1,0:T(8,128)}, u32[]{:S(2)}, u32[]{:S(2)}) collective-permute-start(f32[1,64,128]{2,1,0:T(8,128)} %get-tuple-element.244), channel_id=1, source_target_pairs={{0,16},{16,32},{32,48},{48,64},{64,80},{80,96},{96,112},{112,128},... | collective-permute-start | bytes 98312 | tf_op jit(solution)/shard_map/ppermute | solution.py:26
  13.0 37.3 %collective-permute-start.8 = (f32[1,64,128]{2,1,0:T(8,128)}, f32[1,64,128]{2,1,0:T(8,128)S(1)}, u32[]{:S(2)}, u32[]{:S(2)}) collective-permute-start(f32[1,64,128]{2,1,0:T(8,128)} %get-tuple-element.245), channel_id=1, source_target_pairs={{16,0},{32,16},{48,32},{64,48},{80,64},{96,80},{112,96},{128,112},... | collective-permute-start | bytes 98312 | tf_op jit(solution)/shard_map/ppermute | solution.py:29
  20.3 22.8 %collective-permute-start.6 = (f32[1,64,128]{2,1,0:T(8,128)}, f32[1,64,128]{2,1,0:T(8,128)S(1)}, u32[]{:S(2)}, u32[]{:S(2)}) collective-permute-start(f32[1,64,128]{2,1,0:T(8,128)} %get-tuple-element.246), channel_id=1, source_target_pairs={{0,16},{16,32},{32,48},{48,64},{64,80},{80,96},{96,112},{112,128},... | collective-permute-start | bytes 98312 | tf_op jit(solution)/shard_map/ppermute | solution.py:26
  29.7 12.4 %copy-start.31 = (f32[4,128]{1,0:T(4,128)S(1)}, f32[4,128]{1,0:T(4,128)}, u32[]{:S(2)}) copy-start(f32[4,128]{1,0:T(4,128)} %param.48) | copy-start | bytes 6148
  30.8 106.7 %collective-permute-start = (f32[19,1,16,256]{3,1,2,0:T(1,128)}, f32[19,1,16,256]{3,1,2,0:T(1,128)S(1)}, u32[]{:S(2)}, u32[]{:S(2)}) collective-permute-start(f32[19,1,16,256]{3,1,2,0:T(1,128)} %copy.97), channel_id=1, source_target_pairs={{0,16},{16,32},{32,48},{48,64},{64,80},{80,96},{96,112},{112,128},... | collective-permute-start | bytes 933896 | tf_op jit(solution)/shard_map/ppermute | solution.py:26
  32.8 66.2 %copy-start.4 = (f32[4,63,128]{2,1,0:T(8,128)}, f32[4,63,128]{2,1,0:T(8,128)S(1)}, u32[]{:S(2)}) copy-start(f32[4,63,128]{2,1,0:T(8,128)S(1)} %get-tuple-element.196) | copy-start | bytes 387076
  43.1 60.5 %copy-start.12 = (f32[1,64,128]{2,1,0:T(8,128)}, f32[1,64,128]{2,1,0:T(8,128)S(1)}, u32[]{:S(2)}) copy-start(f32[1,64,128]{2,1,0:T(8,128)S(1)} %collective-permute-done.6) | copy-start | bytes 98308
  43.1 94.4 %collective-permute-start.1 = (f32[19,1,16,256]{3,1,2,0:T(1,128)}, f32[19,1,16,256]{3,1,2,0:T(1,128)S(1)}, u32[]{:S(2)}, u32[]{:S(2)}) collective-permute-start(f32[19,1,16,256]{3,1,2,0:T(1,128)} %copy.99), channel_id=1, source_target_pairs={{16,0},{32,16},{48,32},{64,48},{80,64},{96,80},{112,96},{128,112},... | collective-permute-start | bytes 933896 | tf_op jit(solution)/shard_map/ppermute | solution.py:29
  51.3 40.7 %collective-permute-start.12 = (f32[6,64,1]{2,1,0:T(8,128)S(1)}, f32[6,64,1]{2,1,0:T(8,128)S(1)}, u32[]{:S(2)}, u32[]{:S(2)}) collective-permute-start(f32[6,64,1]{2,1,0:T(8,128)S(1)} %get-tuple-element.239), channel_id=1, source_target_pairs={{1,0},{2,1},{3,2},{4,3},{5,4},{6,5},{7,6},{8,7},{9,8},{10,9},{11,1... | collective-permute-start | bytes 4616 | tf_op jit(solution)/shard_map/ppermute | solution.py:29
  55.2 43.8 %collective-permute-start.10 = (f32[6,64,1]{2,1,0:T(8,128)S(1)}, f32[6,64,1]{2,1,0:T(8,128)S(1)}, u32[]{:S(2)}, u32[]{:S(2)}) collective-permute-start(f32[6,64,1]{2,1,0:T(8,128)S(1)} %get-tuple-element.240), channel_id=1, source_target_pairs={{0,1},{1,2},{2,3},{3,4},{4,5},{5,6},{6,7},{7,8},{8,9},{9,10},{10,1... | collective-permute-start | bytes 4616 | tf_op jit(solution)/shard_map/ppermute | solution.py:26
  61.2 37.9 %collective-permute-start.11 = (f32[6,64,1]{2,1,0:T(8,128)S(1)}, f32[6,64,1]{2,1,0:T(8,128)S(1)}, u32[]{:S(2)}, u32[]{:S(2)}) collective-permute-start(f32[6,64,1]{2,1,0:T(8,128)S(1)} %get-tuple-element.237), channel_id=1, source_target_pairs={{0,1},{1,2},{2,3},{3,4},{4,5},{5,6},{6,7},{7,8},{8,9},{9,10},{10,1... | collective-permute-start | bytes 4616 | tf_op jit(solution)/shard_map/ppermute | solution.py:26
  92.0 12.6 %copy-start.28 = (f32[4,128]{1,0:T(4,128)S(1)}, f32[4,128]{1,0:T(4,128)}, u32[]{:S(2)}) copy-start(f32[4,128]{1,0:T(4,128)} %param.47) | copy-start | bytes 6148
  92.0 11.6 %collective-permute-start.13 = (f32[6,64,1]{2,1,0:T(8,128)S(1)}, f32[6,64,1]{2,1,0:T(8,128)S(1)}, u32[]{:S(2)}, u32[]{:S(2)}) collective-permute-start(f32[6,64,1]{2,1,0:T(8,128)S(1)} %get-tuple-element.238), channel_id=1, source_target_pairs={{1,0},{2,1},{3,2},{4,3},{5,4},{6,5},{7,6},{8,7},{9,8},{10,9},{11,1... | collective-permute-start | bytes 4616 | tf_op jit(solution)/shard_map/ppermute | solution.py:29
  104.7 9.9 %copy-start.6 = (f32[4,64,128]{2,1,0:T(8,128)}, f32[4,64,128]{2,1,0:T(8,128)S(1)}, u32[]{:S(2)}) copy-start(f32[4,64,128]{2,1,0:T(8,128)S(1)} %scatter-add.20) | copy-start | bytes 393220
  105.4 10.8 %collective-permute-start.14 = (f32[1,64,128]{2,1,0:T(8,128)}, f32[1,64,128]{2,1,0:T(8,128)}, u32[]{:S(2)}, u32[]{:S(2)}) collective-permute-start(f32[1,64,128]{2,1,0:T(8,128)} %get-tuple-element.241), channel_id=1, source_target_pairs={{0,16},{16,32},{32,48},{48,64},{64,80},{80,96},{96,112},{112,128},... | collective-permute-start | bytes 98312 | tf_op jit(solution)/shard_map/ppermute | solution.py:26
  107.3 9.1 %collective-permute-start.15 = (f32[1,64,128]{2,1,0:T(8,128)}, f32[1,64,128]{2,1,0:T(8,128)}, u32[]{:S(2)}, u32[]{:S(2)}) collective-permute-start(f32[1,64,128]{2,1,0:T(8,128)} %get-tuple-element.242), channel_id=1, source_target_pairs={{16,0},{32,16},{48,32},{64,48},{80,64},{96,80},{112,96},{128,112},... | collective-permute-start | bytes 98312 | tf_op jit(solution)/shard_map/ppermute | solution.py:29
  116.1 10.0 %copy-start.5 = (f32[4,63,128]{2,1,0:T(8,128)S(1)}, f32[4,63,128]{2,1,0:T(8,128)}, u32[]{:S(2)}) copy-start(f32[4,63,128]{2,1,0:T(8,128)} %copy-done.4) | copy-start | bytes 387076
  116.1 14.6 %copy-start.8 = (f32[4,64,128]{2,1,0:T(8,128)S(1)}, f32[4,64,128]{2,1,0:T(8,128)}, u32[]{:S(2)}) copy-start(f32[4,64,128]{2,1,0:T(8,128)} %copy-done.7) | copy-start | bytes 393220
  116.1 14.6 %copy-start.10 = (f32[4,64,128]{2,1,0:T(8,128)S(1)}, f32[4,64,128]{2,1,0:T(8,128)}, u32[]{:S(2)}) copy-start(f32[4,64,128]{2,1,0:T(8,128)} %copy-done.9) | copy-start | bytes 393220
  116.1 14.6 %copy-start.13 = (f32[1,64,128]{2,1,0:T(8,128)S(1)}, f32[1,64,128]{2,1,0:T(8,128)}, u32[]{:S(2)}) copy-start(f32[1,64,128]{2,1,0:T(8,128)} %copy-done.12) | copy-start | bytes 98308
  117.3 10.0 %collective-permute-start.16 = (f32[6,64,1]{2,1,0:T(8,128)S(1)}, f32[6,64,1]{2,1,0:T(8,128)S(1)}, u32[]{:S(2)}, u32[]{:S(2)}) collective-permute-start(f32[6,64,1]{2,1,0:T(8,128)S(1)} %get-tuple-element.235), channel_id=1, source_target_pairs={{0,1},{1,2},{2,3},{3,4},{4,5},{5,6},{6,7},{7,8},{8,9},{9,10},{10,1... | collective-permute-start | bytes 4616 | tf_op jit(solution)/shard_map/ppermute | solution.py:26
  119.3 11.5 %collective-permute-start.17 = (f32[6,64,1]{2,1,0:T(8,128)S(1)}, f32[6,64,1]{2,1,0:T(8,128)S(1)}, u32[]{:S(2)}, u32[]{:S(2)}) collective-permute-start(f32[6,64,1]{2,1,0:T(8,128)S(1)} %get-tuple-element.236), channel_id=1, source_target_pairs={{1,0},{2,1},{3,2},{4,3},{5,4},{6,5},{7,6},{8,7},{9,8},{10,9},{11,1... | collective-permute-start | bytes 4616 | tf_op jit(solution)/shard_map/ppermute | solution.py:29
  144.1 10.7 %collective-permute-start.2 = (f32[19,6,16,1]{0,2,3,1:T(8,128)S(1)}, f32[19,6,16,1]{0,2,3,1:T(8,128)S(1)}, u32[]{:S(2)}, u32[]{:S(2)}) collective-permute-start(f32[19,6,16,1]{0,2,3,1:T(8,128)S(1)} %copy.102), channel_id=1, source_target_pairs={{0,2},{2,4},{4,6},{6,8},{8,10},{10,12},{12,14},{14,0},{1,3},{3,5},... | collective-permute-start | bytes 21896 | tf_op jit(solution)/shard_map/ppermute | solution.py:26
  146.0 6.5 %collective-permute-start.3 = (f32[19,6,16,1]{0,2,3,1:T(8,128)S(1)}, f32[19,6,16,1]{0,2,3,1:T(8,128)S(1)}, u32[]{:S(2)}, u32[]{:S(2)}) collective-permute-start(f32[19,6,16,1]{0,2,3,1:T(8,128)S(1)} %copy.104), channel_id=1, source_target_pairs={{2,0},{4,2},{6,4},{8,6},{10,8},{12,10},{14,12},{0,14},{3,1},{5,3},... | collective-permute-start | bytes 21896 | tf_op jit(solution)/shard_map/ppermute | solution.py:29
  157.6 23.4 %collective-permute-start.5 = (f32[19,6,1,258]{3,1,2,0:T(8,128)S(1)}, f32[19,6,1,258]{3,1,2,0:T(8,128)S(1)}, u32[]{:S(2)}, u32[]{:S(2)}) collective-permute-start(f32[19,6,1,258]{3,1,2,0:T(8,128)S(1)} %get-tuple-element.210), channel_id=1, source_target_pairs={{1,0},{0,1},{3,2},{2,3},{5,4},{4,5},{7,6},{6,7},{9,8},{8,9},{11,10... | collective-permute-start | bytes 352952 | tf_op jit(solution)/shard_map/ppermute | solution.py:29
  162.5 6.6 %copy-start = (f32[19,6,16,1]{3,1,2,0:T(8,128)S(1)}, f32[19,6,16,1]{3,1,2,0:T(8,128)}, u32[]{:S(2)}) copy-start(f32[19,6,16,1]{3,1,2,0:T(8,128)} %copy.105) | copy-start | bytes 21892
  162.5 22.7 %collective-permute-start.4 = (f32[19,6,1,258]{3,1,2,0:T(8,128)S(1)}, f32[19,6,1,258]{3,1,2,0:T(8,128)S(1)}, u32[]{:S(2)}, u32[]{:S(2)}) collective-permute-start(f32[19,6,1,258]{3,1,2,0:T(8,128)S(1)} %get-tuple-element.211), channel_id=1, source_target_pairs={{0,1},{1,0},{2,3},{3,2},{4,5},{5,4},{6,7},{7,6},{8,9},{9,8},{10,11... | collective-permute-start | bytes 352952 | tf_op jit(solution)/shard_map/ppermute | solution.py:26
  191.6 9.8 %copy-start.20 = (f32[1,4,16,256]{3,2,1,0:T(8,128)S(1)}, f32[1,4,16,256]{3,2,1,0:T(8,128)}, u32[]{:S(2)}) copy-start(f32[1,4,16,256]{3,2,1,0:T(8,128)} %copy.118) | copy-start | bytes 196612
  191.6 10.5 %copy-start.18 = (f32[1,4,16,256]{3,2,1,0:T(8,128)S(1)}, f32[1,4,16,256]{3,2,1,0:T(8,128)}, u32[]{:S(2)}) copy-start(f32[1,4,16,256]{3,2,1,0:T(8,128)} %scatter.49) | copy-start | bytes 196612
  (20 other events, 58.0 us)
where the time goes:
time: 204 us; the launch traced here: 203 us
  starting transfers between devices  86.5 us (42%)
  waiting for transfers between devices  43.1 us (21%)
  local copies, waits for them, and re-layouts  39.2 us (19%)
  other arithmetic  17.9 us (9%)
  blocking collectives  9.22 us (5%)
  matrix products  5.46 us (3%)
    ppermute x9, starting transfers between devices, padded_2(): lax.ppermute(lax.slice_in_dim(block, 0, width, axis=dim), axis, backward)  56.4 us
    ppermute x9, waiting for transfers between devices, padded_2(): lax.ppermute(lax.slice_in_dim(block, 0, width, axis=dim), axis, backward)  41.8 us
    ppermute x9, starting transfers between devices, padded_2(): lax.ppermute(lax.slice_in_dim(block, block.shape[dim] - width, None, axis...  30 us
    unnamed x96, local copies, waits for them, and re-layouts  17.2 us
    psum x1, blocking collectives, broadcast(): return lax.psum(block, axis)  9.22 us
    slice x7, local copies, waits for them, and re-layouts, padded_2(): lax.slice_in_dim(block, 0, width, axis=dim)  7.93 us
    concatenate x6, other arithmetic, padded_2(): block = jnp.concatenate([low, block, high], axis=dim)  5.27 us
  transfers between devices with their start and end apart: 18, of which 7 were waited for; matrix products, arithmetic and copies ran while one was open for 16% of the time, Pallas kernels for 0%

commit v1 on v0

v1 whole, which is shorter than its diff:
```python
import jax
import jax.numpy as jnp
from jax import lax
from jax.experimental import pallas as pl
from jax.experimental.pallas import tpu as pltpu
from jax.sharding import PartitionSpec as P

F32 = jnp.float32
JET_SPEED = 0.1
H_BASE = 0.5
H_GAIN = 40.0
SHEAR_RATE = 1.6
ODD_RATE = 1.2
EVEN_RATE = 1.4
VEL = (
    (0, 0, 0),
    (1, 0, 0), (-1, 0, 0), (0, 1, 0), (0, -1, 0), (0, 0, 1), (0, 0, -1),
    (1, 1, 0), (-1, -1, 0), (1, -1, 0), (-1, 1, 0),
    (1, 0, 1), (-1, 0, -1), (1, 0, -1), (-1, 0, 1),
    (0, 1, 1), (0, -1, -1), (0, 1, -1), (0, -1, 1),
)
OPP = tuple(VEL.index(tuple(-e for e in v)) for v in VEL)
WEIGHT = (1.0 / 3.0,) + (1.0 / 18.0,) * 6 + (1.0 / 36.0,) * 12
X_UP, X_DN = (1, 7, 9, 11, 13), (2, 10, 8, 14, 12)
Y_UP, Y_DN = (3, 7, 10, 15, 17), (4, 9, 8, 18, 16)
Z_UP, Z_DN = (5, 11, 14, 15, 18), (6, 13, 12, 17, 16)
SX, SZ_, HALF = 4, 16, 128
DEPTH = 64
Z_S, Z_E, Z_ROWS = 40, 56, 64
Y_S, Y_E, Y_D, Y_ROWS = 16, 32, 40, 48
X_U, X_SL, X_SR, X_YP, X_YM, X_R, X_ROWS = 160, 416, 432, 448, 464, 480, 488


def roll(value, shift, axis):
    size = value.shape[axis]
    shift = shift % size
    return value if shift == 0 else pltpu.roll(value, shift, axis)


def lanes(shape):
    return lax.broadcasted_iota(jnp.int32, shape, len(shape) - 1)


def rows_of(shape):
    return lax.broadcasted_iota(jnp.int32, shape, 0)


def collide(f):
    s = {i: f[i] + f[i + 1] for i in range(1, 19, 2)}
    d = {i: f[i] - f[i + 1] for i in range(1, 19, 2)}
    s_ab, s_ac, s_bc = s[7] + s[9], s[11] + s[13], s[15] + s[17]
    rho = (f[0] + s[1]) + (s[3] + s[5]) + (s_ab + s_ac + s_bc)
    m_a = d[1] + (d[7] + d[9]) + (d[11] + d[13])
    m_b = d[3] + (d[7] - d[9]) + (d[15] + d[17])
    m_c = d[5] + (d[11] - d[13]) + (d[15] - d[17])
    inv = 1.0 / rho
    u_a, u_b, u_c = m_a * inv, m_b * inv, m_c * inv
    p_aa, p_bb, p_cc = m_a * u_a, m_b * u_b, m_c * u_c
    p_ab, p_ac, p_bc = m_a * u_b, m_a * u_c, m_b * u_c
    q = p_aa + p_bb + p_cc
    base = rho - 1.5 * q
    t = rho - 2.0 * q
    t_ab = 4.0 * f[0] - 2.0 * (s[1] + s[3]) + s_ab - (t + 0.5 * p_cc)
    t_ac = 4.0 * f[0] - 2.0 * (s[1] + s[5]) + s_ac - (t + 0.5 * p_bb)
    t_bc = 4.0 * f[0] - 2.0 * (s[3] + s[5]) + s_bc - (t + 0.5 * p_aa)
    mean = (2.0 / 7.0) * (t_ab + t_ac + t_bc)
    gain = (SHEAR_RATE - EVEN_RATE) / 12.0
    c_ab, c_ac, c_bc = gain * (t_ab - mean), gain * (t_ac - mean), gain * (t_bc - mean)
    keep, half_keep, half = 1.0 - SHEAR_RATE, 0.5 * (1.0 - SHEAR_RATE), 0.5 * SHEAR_RATE
    odd, pull = 0.5 * (1.0 - ODD_RATE), 3.0 * ODD_RATE
    post = [None] * 19
    post[0] = keep * f[0] + (SHEAR_RATE / 3.0) * base + 4.0 * (c_ab + c_ac + c_bc)

    def put(i, extra, equil, moment, weight):
        even = half_keep * s[i] + equil + extra
        anti = odd * d[i] + (pull * weight) * moment
        post[i] = even + anti
        post[i + 1] = even - anti

    axis = half / 9.0
    for i, p, c, m in ((1, p_aa, c_ab + c_ac, m_a), (3, p_bb, c_ab + c_bc, m_b), (5, p_cc, c_ac + c_bc, m_c)):
        put(i, -2.0 * c, axis * (base + 4.5 * p), m, 1.0 / 18.0)
    diag = half / 18.0
    for i, pp, pq, c, m, n in (
        (7, p_aa + p_bb, p_ab, c_ab, m_a, m_b),
        (11, p_aa + p_cc, p_ac, c_ac, m_a, m_c),
        (15, p_bb + p_cc, p_bc, c_bc, m_b, m_c),
    ):
        even = diag * (base + 4.5 * pp)
        cross = (9.0 * diag) * pq
        put(i, c, even + cross, m + n, 1.0 / 36.0)
        put(i + 2, c, even - cross, m - n, 1.0 / 36.0)
    return post, q * inv


def collide_kernel(pops, temp, cond, load, cool, post, zbuf, yp, ym, xp, xm, own, heat, buf, sems):
    copies = [pltpu.make_async_copy(pops.at[:, x], buf.at[:, x], sems.at[x]) for x in range(SX)]
    for copy in copies:
        copy.start()
    low = lax.axis_index("gz") == 0
    lane = lanes((DEPTH, HALF))
    edges = jnp.zeros((DEPTH, HALF), F32)
    for k, field in enumerate((temp, cond)):
        for x in range(SX):
            at = k * 16 + x * 4
            edges = jnp.where((lane >= at) & (lane < at + 4), roll(field[x], at + 2, 1), edges)
    own[...] = edges
    lane16 = lanes((16, HALF))
    fold = edges[0:16]
    for g in range(1, 4):
        fold = jnp.where(lane16 >= 32 * g, roll(edges[16 * g : 16 * g + 16], 32 * g, 1), fold)
    zbuf[Z_S : Z_S + 16, :] = fold
    for k, field in enumerate((temp, cond)):
        for buffer, near, far in ((xp, 3, 2), (xm, 0, 1)):
            at = X_U + 128 * k
            buffer[at : at + 64, :] = field[near]
            buffer[at + 64 : at + 128, :] = field[far]
    y_up = [jnp.zeros((8, HALF), F32) for _ in range(2)]
    y_dn = [jnp.zeros((8, HALF), F32) for _ in range(2)]
    lane8 = lanes((8, HALF))
    for x in range(SX):
        copies[x].wait()
        for k in range(2):
            z = slice(8 * k, 8 * k + 8)
            for h in range(2):
                y = slice(HALF * h, HALF * h + HALF)
                out, speed = collide([buf[v, x, z, y] for v in range(19)])
                for v in range(19):
                    post[v, x, z, y] = out[v]
                if k == 0:
                    heat[4 * h + x : 4 * h + x + 1, :] = H_BASE + H_GAIN * speed[0:1, :]
                for n in range(5):
                    row = 20 * h + 4 * n + x
                    if k == 0:
                        zbuf[row : row + 1, :] = out[Z_DN[n]][0:1, :]
                    else:
                        down = zbuf[row : row + 1, :]
                        zbuf[row : row + 1, :] = jnp.where(low, out[Z_UP[n]][7:8, :], down)
                    at = 4 * n + x
                    if h == 1:
                        y_up[k] = jnp.where(lane8 == at, roll(out[Y_UP[n]], at - 127, 1), y_up[k])
                    else:
                        y_dn[k] = jnp.where(lane8 == at, roll(out[Y_DN[n]], at, 1), y_dn[k])
                    at = 32 * n + 16 * h + 8 * k
                    if x == 3:
                        xp[at : at + 8, :] = out[X_UP[n]]
                    if x == 0:
                        xm[at : at + 8, :] = out[X_DN[n]]
    for k in range(2):
        yp[8 * k : 8 * k + 8, :] = y_up[k]
        ym[8 * k : 8 * k + 8, :] = y_dn[k]
    lane1 = lanes((1, HALF))
    row = jnp.zeros((1, HALF), F32)
    for k, (field, first) in enumerate(((load, 0), (cool, 0), (heat, 0), (heat, 4))):
        for x in range(SX):
            at = k * 16 + x * 4
            value = field[first + x : first + x + 1, :]
            row = jnp.where((lane1 >= at) & (lane1 < at + 2), roll(value, at + 1, 1), row)
    zbuf[Z_E : Z_E + 4, :] = heat[4:8, :]
    zbuf[Z_E + 4 : Z_E + 5, :] = row
    zbuf[Z_E + 5 : Z_E + 8, :] = jnp.zeros((3, HALF), F32)


def y_kernel(yp, ym, zbuf, zin, outp, outm):
    low = lax.axis_index("gz") == 0
    lane = lanes((1, HALF))
    sent = zin[Z_E + 4 : Z_E + 5, :]
    row = jnp.where((lane >= 32) & low, zbuf[Z_E + 4 : Z_E + 5, :], sent)
    for out, edge, first in ((outp, yp, 20 + 12), (outm, ym, 16)):
        out[0:16, :] = edge[...]
        out[Y_S : Y_S + 16, :] = zin[Z_S : Z_S + 16, :]
        out[Y_E : Y_E + 8, :] = jnp.broadcast_to(row, (8, HALF))
        out[Y_D : Y_D + 4, :] = zin[first : first + 4, :]
        out[Y_D + 4 : Y_D + 8, :] = jnp.zeros((4, HALF), F32)


def x_kernel(inp, inm, zin, ypin, ymin, load, cool, heat, outp, outm, tail, sems):
    low = lax.axis_index("gz") == 0
    left = jnp.where(low, ypin[Y_S : Y_S + 16, :], zin[Z_S : Z_S + 16, :])
    right = jnp.where(low, zin[Z_S : Z_S + 16, :], ymin[Y_S : Y_S + 16, :])
    warm = jnp.where(low, heat[0:4, :], zin[Z_E : Z_E + 4, :])
    copies = []
    for k, (out, x, n) in enumerate(((outp, 3, 1), (outm, 0, 2))):
        part = tail.at[k]
        part[0:16, :] = left
        part[16:32, :] = right
        part[32:48, :] = ypin[0:16, :]
        part[48:64, :] = ymin[0:16, :]
        for h in range(2):
            row = 20 * h + 4 * n + x
            part[64 + h : 65 + h, :] = zin[row : row + 1, :]
        part[66:67, :] = load[x : x + 1, :]
        part[67:68, :] = cool[x : x + 1, :]
        part[68:69, :] = warm[x : x + 1, :]
        part[69:72, :] = jnp.zeros((3, HALF), F32)
        copies.append(pltpu.make_async_copy(part, out.at[X_SL:X_ROWS], sems.at[k]))
    for copy in copies:
        copy.start()
    for copy in copies:
        copy.wait()


def final_kernel(
    post, zin, ypin, ymin, xpin, xmin, nozzle, wall, temp, cond, load, cool, own, heat, zbuf,
    pops_out, solid_out,
):
    low = lax.axis_index("gz") == 0
    lane = lanes((SZ_, HALF))
    layer = rows_of((SZ_, HALF))
    for v, (a, b, c) in enumerate(VEL):
        for x in range(SX):
            s = x - a
            inside = 0 <= s < SX
            edge = xpin if s < 0 else xmin
            if inside:
                tiles = [post[v, s, :, HALF * h : HALF * h + HALF] for h in range(2)]
            else:
                n = (X_UP if s < 0 else X_DN).index(v)
                tiles = [edge[32 * n + 16 * h : 32 * n + 16 * h + 16, :] for h in range(2)]
            beside = None
            if b:
                slab, first = (ypin, X_YP) if b > 0 else (ymin, X_YM)
                k = 4 * (Y_UP if b > 0 else Y_DN).index(v) + (s if inside else (3 if s < 0 else 0))
                to = 0 if b > 0 else HALF - 1
                column = slab[0:16, :] if inside else edge[first : first + 16, :]
                beside = roll(column, to - k, 1)
            if c:
                n = (Z_UP if c > 0 else Z_DN).index(v)
                at = 0 if c > 0 else SZ_ - 1
                for h in range(2):
                    row = zin[20 * h + 4 * n + s : 20 * h + 4 * n + s + 1, :] if inside else edge[X_R + h : X_R + h + 1, :]
                    tiles[h] = jnp.where(layer == at, row, roll(tiles[h], c, 0))
                if b:
                    corner = roll(slab[Y_D + x : Y_D + x + 1, :], b, 1)
                    beside = jnp.where(layer == at, corner, roll(beside, c, 0))
            if b > 0:
                t0, t1 = roll(tiles[0], 1, 1), roll(tiles[1], 1, 1)
                tiles = [jnp.where(lane == 0, beside, t0), jnp.where(lane == 0, t0, t1)]
            elif b < 0:
                t0, t1 = roll(tiles[0], -1, 1), roll(tiles[1], -1, 1)
                tiles = [jnp.where(lane == HALF - 1, t1, t0), jnp.where(lane == HALF - 1, beside, t1)]
            for h in range(2):
                y = slice(HALF * h, HALF * h + HALF)
                if c > 0:
                    back = post[OPP[v], x, 0:1, y]
                    tiles[h] = jnp.where((layer == 0) & low, back, tiles[h])
                elif c < 0:
                    back = post[OPP[v], x, SZ_ - 1 : SZ_, y]
                    through = post[v, x, SZ_ - 1 : SZ_, y]
                    top = jnp.where(
                        nozzle[x : x + 1, y] == 1,
                        back + 6.0 * WEIGHT[v] * JET_SPEED,
                        jnp.where(wall[x : x + 1, y] == 1, through, back),
                    )
                    tiles[h] = jnp.where((layer == SZ_ - 1) & jnp.logical_not(low), top, tiles[h])
                pops_out[v, x, :, y] = tiles[h]

    lane = lanes((DEPTH, HALF))
    depth = rows_of((DEPTH, HALF))
    floor, face = depth == 0, depth == DEPTH - 1

    def spread(folded, at):
        return jnp.concatenate([roll(folded, at - 32 * g, 1) for g in range(4)], axis=0)

    def vertical(c):
        down = jnp.where(face, 0.0, 0.5 * (c + roll(c, -1, 0)))
        return down, roll(down, 1, 0)

    def around(u, links):
        total = None
        for link, near in links:
            total = link * near if total is None else total + link * near
        return total

    U = {x: temp[x] for x in range(SX)}
    C = {x: cond[x] for x in range(SX)}
    for near, far, edge in ((-1, -2, xpin), (4, 5, xmin)):
        U[near], U[far] = edge[X_U : X_U + 64, :], edge[X_U + 64 : X_U + 128, :]
        C[near], C[far] = edge[X_U + 128 : X_U + 192, :], edge[X_U + 192 : X_U + 256, :]
    warm = jnp.where(low, heat[0:4, :], zin[Z_E : Z_E + 4, :])
    loads = {x: load[x : x + 1, :] for x in range(SX)}
    cools = {x: cool[x : x + 1, :] for x in range(SX)}
    warms = {x: warm[x : x + 1, :] for x in range(SX)}
    for x, edge in ((-1, xpin), (4, xmin)):
        loads[x], cools[x], warms[x] = (edge[X_R + 2 + k : X_R + 3 + k, :] for k in range(3))

    left = jnp.where(low, ypin[Y_S : Y_S + 16, :], zin[Z_S : Z_S + 16, :])
    right = jnp.where(low, zin[Z_S : Z_S + 16, :], ymin[Y_S : Y_S + 16, :])
    own_edges = own[...]
    near_first = {}
    side = {}
    row_left = jnp.where(low, ypin[Y_E : Y_E + 1, :], zin[Z_E + 4 : Z_E + 5, :])
    row_right = jnp.where(low, zin[Z_E + 4 : Z_E + 5, :], ymin[Y_E : Y_E + 1, :])
    heat_left = jnp.where(low, roll(row_left, -48, 1), roll(row_left, -32, 1))
    heat_right = jnp.where(low, roll(zbuf[Z_E + 4 : Z_E + 5, :], -49, 1), roll(row_right, -33, 1))
    for name, folded, at, j1, j2, jo, row, h_row, jr in (
        ("left", left, X_SL, 1, 0, 2, row_left, heat_left, 0),
        ("right", right, X_SR, 2, 3, 1, row_right, heat_right, 1),
    ):
        u1, u2 = spread(folded, -j1), spread(folded, -j2)
        c1, c2 = spread(folded, -16 - j1), spread(folded, -16 - j2)
        before, after = xpin[at : at + 16, :], xmin[at : at + 16, :]
        u1 = jnp.where(lane == 124, spread(before, 124 - 12 - j1), jnp.where(lane == 16, spread(after, 16 - j1), u1))
        c1 = jnp.where(lane == 124, spread(before, 124 - 28 - j1), jnp.where(lane == 16, spread(after, -j1), c1))
        side[name] = (u1, c1)
        uo, co = roll(own_edges, -jo, 1), roll(own_edges, -16 - jo, 1)
        g_far, g_own = 0.5 * (c1 + c2), 0.5 * (c1 + co)
        g_up = 0.5 * (c1 + roll(c1, -4, 1))
        g_dn = roll(g_up, 4, 1)
        v_dn, v_up = vertical(c1)
        e_load, e_cool = roll(row, -jr, 1), roll(row, -16 - jr, 1)
        num = u1 + jnp.where(floor, e_load, 0.0) + jnp.where(face, h_row * e_cool, 0.0)
        den = 1.0 + jnp.where(face, h_row, 0.0) + (g_far + g_own) + (g_up + g_dn) + (v_dn + v_up)
        num = num + around(u1, ((g_far, u2), (g_own, uo), (g_up, roll(u1, -4, 1)), (g_dn, roll(u1, 4, 1)),
                                (v_dn, roll(u1, -1, 0)), (v_up, roll(u1, 1, 0))))
        near_first[name] = num / den

    def beside_of(value, left_col, right_col):
        return (
            jnp.where(lane == 0, left_col, roll(value, 1, 1)),
            jnp.where(lane == HALF - 1, right_col, roll(value, -1, 1)),
        )

    def columns(pair, x):
        at = (4 * x) % HALF
        return roll(pair[0], -at, 1), roll(pair[1], HALF - 1 - at, 1)

    pair_u = (side["left"][0], side["right"][0])
    pair_c = (side["left"][1], side["right"][1])
    pair_f = (near_first["left"], near_first["right"])
    g_x = {x: 0.5 * (C[x] + C[x + 1]) for x in range(-2, 5)}
    first, kept = {}, {}
    for x in range(-1, 5):
        c_l, c_r = beside_of(C[x], *columns(pair_c, x))
        u_l, u_r = beside_of(U[x], *columns(pair_u, x))
        g_l, g_r = 0.5 * (C[x] + c_l), 0.5 * (C[x] + c_r)
        v_dn, v_up = vertical(C[x])
        base = U[x] + jnp.where(floor, loads[x], 0.0) + jnp.where(face, warms[x] * cools[x], 0.0)
        den = 1.0 + jnp.where(face, warms[x], 0.0) + (g_x[x - 1] + g_x[x]) + (g_l + g_r) + (v_dn + v_up)
        inv = 1.0 / den
        num = base + around(U[x], ((g_x[x - 1], U[x - 1]), (g_x[x], U[x + 1]), (g_l, u_l), (g_r, u_r),
                                   (v_dn, roll(U[x], -1, 0)), (v_up, roll(U[x], 1, 0))))
        first[x] = num * inv
        kept[x] = (base, inv, g_l, g_r, v_dn, v_up)
    for x in range(SX):
        base, inv, g_l, g_r, v_dn, v_up = kept[x]
        f_l, f_r = beside_of(first[x], *columns(pair_f, x))
        num = base + around(first[x], ((g_x[x - 1], first[x - 1]), (g_x[x], first[x + 1]), (g_l, f_l), (g_r, f_r),
                                       (v_dn, roll(first[x], -1, 0)), (v_up, roll(first[x], 1, 0))))
        solid_out[x] = num * inv


def shape(*dims):
    return jax.ShapeDtypeStruct(dims, F32)


VM = pl.BlockSpec(memory_space=pltpu.VMEM)
ANY = pl.BlockSpec(memory_space=pl.ANY)


def ring(axis, step):
    n = lax.axis_size(axis)
    return [(i, (i + step) % n) for i in range(n)]


def body(populations, nozzle_mask, wall_type, solid_temp, diffusion, heat_load, coolant_temp):
    post, zbuf, yp, ym, xp, xm, own, heat = pl.pallas_call(
        collide_kernel,
        name="collide",
        in_specs=[ANY, VM, VM, VM, VM],
        out_specs=[VM] * 8,
        out_shape=[
            shape(19, SX, SZ_, 2 * HALF), shape(Z_ROWS, HALF), shape(16, HALF), shape(16, HALF),
            shape(X_ROWS, HALF), shape(X_ROWS, HALF), shape(DEPTH, HALF), shape(8, HALF),
        ],
        scratch_shapes=[pltpu.VMEM((19, SX, SZ_, 2 * HALF), F32), pltpu.SemaphoreType.DMA((SX,))],
    )(populations, solid_temp, diffusion, heat_load, coolant_temp)
    zin = lax.ppermute(zbuf, "gz", ring("gz", 1))
    ypo, ymo = pl.pallas_call(
        y_kernel,
        name="pack_y",
        in_specs=[VM] * 4,
        out_specs=[VM] * 2,
        out_shape=[shape(Y_ROWS, HALF)] * 2,
    )(yp, ym, zbuf, zin)
    ypin = lax.ppermute(ypo, "gy", ring("gy", 1))
    ymin = lax.ppermute(ymo, "gy", ring("gy", -1))
    xpo, xmo = pl.pallas_call(
        x_kernel,
        name="pack_x",
        in_specs=[ANY] * 2 + [VM] * 6,
        out_specs=[ANY] * 2,
        out_shape=[shape(X_ROWS, HALF)] * 2,
        scratch_shapes=[pltpu.VMEM((2, X_ROWS - X_SL, HALF), F32), pltpu.SemaphoreType.DMA((2,))],
        input_output_aliases={0: 0, 1: 1},
    )(xp, xm, zin, ypin, ymin, heat_load, coolant_temp, heat)
    xpin = lax.ppermute(xpo, "gx", ring("gx", 1))
    xmin = lax.ppermute(xmo, "gx", ring("gx", -1))
    return pl.pallas_call(
        final_kernel,
        name="finish",
        in_specs=[VM] * 15,
        out_specs=[VM] * 2,
        out_shape=[shape(19, SX, SZ_, 2 * HALF), shape(SX, DEPTH, HALF)],
    )(post, zin, ypin, ymin, xpin, xmin, nozzle_mask, wall_type, solid_temp, diffusion,
      heat_load, coolant_temp, own, heat, zbuf)


def solution(mesh):
    placed = (
        P(None, "gx", "gz", "gy"),
        P("gx", "gy"),
        P("gx", "gy"),
        P("gx", None, ("gy", "gz")),
        P("gx", None, ("gy", "gz")),
        P("gx", ("gy", "gz")),
        P("gx", ("gy", "gz")),
    )
    return jax.shard_map(
        body,
        mesh=mesh,
        in_specs=placed,
        out_specs=(P(None, "gx", "gz", "gy"), P("gx", None, ("gy", "gz"))),
        check_vma=False,
    )
```

time: 204 us -> 51.7 us (0.25)
  the two profiles are of different devices: /device:TPU:192 before, /device:TPU:62 now
where the time goes in v1:
time: 51.7 us; the launch traced here: 51.2 us
  starting transfers between devices  24.1 us (47%)
  waiting for transfers between devices  13.4 us (26%)
  Pallas kernels  11 us (21%)
  local copies, waits for them, and re-layouts  1.93 us (4%)
  between operations  0.71 us (1%)
    ppermute x1, starting transfers between devices, body(): zin = lax.ppermute(zbuf, 'gz', ring('gz', 1))  10.9 us
    ppermute x1, waiting for transfers between devices, body(): xmin = lax.ppermute(xmo, 'gx', ring('gx', -1))  5.69 us
    ppermute x1, starting transfers between devices, body(): ymin = lax.ppermute(ymo, 'gy', ring('gy', -1))  5.44 us
    pallas_call x1, Pallas kernels, body(): pl.pallas_call(final_kernel, name='finish', in_specs=[VM] * 15, out_specs...  4.21 us
    pallas_call x1, Pallas kernels, body(): pl.pallas_call(collide_kernel, name='collide', in_specs=[ANY, VM, VM, VM,...  3.96 us
    ppermute x1, waiting for transfers between devices, body(): xpin = lax.ppermute(xpo, 'gx', ring('gx', 1))  3.94 us
    ppermute x1, starting transfers between devices, body(): xpin = lax.ppermute(xpo, 'gx', ring('gx', 1))  3.82 us
    ppermute x1, waiting for transfers between devices, body(): zin = lax.ppermute(zbuf, 'gz', ring('gz', 1))  2.12 us
  transfers between devices with their start and end apart: 5, of which 4 were waited for; matrix products, arithmetic and copies ran while one was open for 0% of the time, Pallas kernels for 0%

profile of v1, /device:TPU:62, one launch (start us, length us, event | category | flops | bytes accessed | tf_op | source)
XLA Modules:
  0.0 51.2 jit_solution(3389749686986312537)
XLA Ops:
  0.6 4.0 %collide.1 = (f32[19,4,16,256]{3,2,1,0:T(8,128)}, f32[64,128]{1,0:T(8,128)}, f32[16,128]{1,0:T(8,128)}, f32[16,128]{1,0:T(8,128)}, f32[488,128]{1,0:T(8,128)}, /...) custom-call(f32[19,4,16,256]{3,2,1,0:T(8,128)} %pops.1, f32[4,64,128]{2,1,0:T(8,128)} %temp.3, ...), custom_call_target="tpu_custom_call" | custom-call | tf_op jit(solution)/shard_map/collide/pallas_call | solution.py:367
  4.6 10.9 %collective-permute-start = (f32[64,128]{1,0:T(8,128)}, f32[64,128]{1,0:T(8,128)S(1)}, u32[]{:S(2)}, u32[]{:S(2)}) collective-permute-start(f32[64,128]{1,0:T(8,128)} %get-tuple-element.15.zbuf), channel_id=1, source_target_pairs={{0,1},{1,0},{2,3},{3,2},{4,5},{5,4},{6,7},{7,6},{8,9},{9,8},{10,11... | collective-permute-start | bytes 98312 | tf_op jit(solution)/shard_map/ppermute | solution.py:378
  15.5 2.1 %collective-permute-done.zin = f32[64,128]{1,0:T(8,128)S(1)} collective-permute-done((f32[64,128]{1,0:T(8,128)}, f32[64,128]{1,0:T(8,128)S(1)}, u32[]{:S(2)}, u32[]{:S(2)}) %collective-permute-start) | collective-permute-done | bytes 32800 | tf_op jit(solution)/shard_map/ppermute | solution.py:378
  17.6 0.0 copy-start
  17.6 0.6 %copy-done = f32[64,128]{1,0:T(8,128)} copy-done((f32[64,128]{1,0:T(8,128)}, f32[64,128]{1,0:T(8,128)S(1)}, u32[]{:S(2)}) %copy-start) | copy-done | bytes 32792
  18.3 1.4 %pack_y.1 = (f32[48,128]{1,0:T(8,128)}, f32[48,128]{1,0:T(8,128)}) custom-call(f32[16,128]{1,0:T(8,128)} %get-tuple-element.16.yp, f32[16,128]{1,0:T(8,128)} %get-tuple-element.17.ym, f32[64,128]{1,0:T(8,128)} %get-tuple-element.15.zbuf, f32[64,128]{1,0:T(8,128)} %copy-done), custom_call_target="tpu_custom_call" | custom-call | tf_op jit(solution)/shard_map/pack_y/pallas_call | solution.py:379
  19.7 1.9 %collective-permute-start.1 = (f32[48,128]{1,0:T(8,128)}, f32[48,128]{1,0:T(8,128)S(1)}, u32[]{:S(2)}, u32[]{:S(2)}) collective-permute-start(f32[48,128]{1,0:T(8,128)} %get-tuple-element.18), channel_id=1, source_target_pairs={{0,2},{2,4},{4,6},{6,8},{8,10},{10,12},{12,14},{14,0},{1,3},{3,5},... | collective-permute-start | bytes 73736 | tf_op jit(solution)/shard_map/ppermute | solution.py:386
  21.6 5.4 %collective-permute-start.2 = (f32[48,128]{1,0:T(8,128)}, f32[48,128]{1,0:T(8,128)S(1)}, u32[]{:S(2)}, u32[]{:S(2)}) collective-permute-start(f32[48,128]{1,0:T(8,128)} %get-tuple-element.19), channel_id=1, source_target_pairs={{0,14},{2,0},{4,2},{6,4},{8,6},{10,8},{12,10},{14,12},{1,15},{3,1}... | collective-permute-start | bytes 73736 | tf_op jit(solution)/shard_map/ppermute | solution.py:387
  27.1 0.0 collective-permute-done.1.ypin
  27.1 0.0 copy-start.3
  27.1 1.7 %collective-permute-done.2.ymin = f32[48,128]{1,0:T(8,128)S(1)} collective-permute-done((f32[48,128]{1,0:T(8,128)}, f32[48,128]{1,0:T(8,128)S(1)}, u32[]{:S(2)}, u32[]{:S(2)}) %collective-permute-start.2) | collective-permute-done | bytes 24608 | tf_op jit(solution)/shard_map/ppermute | solution.py:387
  28.8 0.0 copy-start.4
  28.8 0.0 copy-done.3
  28.8 0.6 %copy-done.4 = f32[48,128]{1,0:T(8,128)} copy-done((f32[48,128]{1,0:T(8,128)}, f32[48,128]{1,0:T(8,128)S(1)}, u32[]{:S(2)}) %copy-start.4) | copy-done | bytes 24600
  29.4 1.4 %pack_x.1 = (f32[488,128]{1,0:T(8,128)}, f32[488,128]{1,0:T(8,128)}) custom-call(f32[488,128]{1,0:T(8,128)} %get-tuple-element.20.inp, f32[488,128]{1,0:T(8,128)} %get-tuple-element.21.inm, f32[64,128]{1,0:T(8,128)} %copy-done, f32[48,128]{1,0:T(8,128)} %copy-done.3, f32[48,128]{1,0:T(8,128)} %copy-done.4, ...), custom_call_target="tpu_custom_call", output_to_operand_aliasing={{0}: (0, {}), {1}: (1, {})} | custom-call | tf_op jit(solution)/shard_map/pack_x/pallas_call | solution.py:388
  30.8 3.8 %collective-permute-start.3 = (f32[488,128]{1,0:T(8,128)}, f32[488,128]{1,0:T(8,128)S(1)}, u32[]{:S(2)}, u32[]{:S(2)}) collective-permute-start(f32[488,128]{1,0:T(8,128)} %get-tuple-element.23), channel_id=1, source_target_pairs={{0,16},{16,32},{32,48},{48,64},{64,80},{80,96},{96,112},{112,128},... | collective-permute-start | bytes 749576 | tf_op jit(solution)/shard_map/ppermute | solution.py:397
  34.7 2.0 %collective-permute-start.4 = (f32[488,128]{1,0:T(8,128)}, f32[488,128]{1,0:T(8,128)S(1)}, u32[]{:S(2)}, u32[]{:S(2)}) collective-permute-start(f32[488,128]{1,0:T(8,128)} %get-tuple-element.24), channel_id=1, source_target_pairs={{0,496},{16,0},{32,16},{48,32},{64,48},{80,64},{96,80},{112,96},{1... | collective-permute-start | bytes 749576 | tf_op jit(solution)/shard_map/ppermute | solution.py:398
  36.7 3.9 %collective-permute-done.3.xpin = f32[488,128]{1,0:T(8,128)S(1)} collective-permute-done((f32[488,128]{1,0:T(8,128)}, f32[488,128]{1,0:T(8,128)S(1)}, u32[]{:S(2)}, u32[]{:S(2)}) %collective-permute-start.3) | collective-permute-done | bytes 249888 | tf_op jit(solution)/shard_map/ppermute | solution.py:397
  40.6 0.0 copy-start.1
  40.6 5.7 %collective-permute-done.4.xmin = f32[488,128]{1,0:T(8,128)S(1)} collective-permute-done((f32[488,128]{1,0:T(8,128)}, f32[488,128]{1,0:T(8,128)S(1)}, u32[]{:S(2)}, u32[]{:S(2)}) %collective-permute-start.4) | collective-permute-done | bytes 249888 | tf_op jit(solution)/shard_map/ppermute | solution.py:398
  46.3 0.0 copy-start.2
  46.3 0.0 copy-done.1
  46.3 0.7 %copy-done.2 = f32[488,128]{1,0:T(8,128)} copy-done((f32[488,128]{1,0:T(8,128)}, f32[488,128]{1,0:T(8,128)S(1)}, u32[]{:S(2)}) %copy-start.2) | copy-done | bytes 249880
  47.0 4.2 %finish.1 = (f32[19,4,16,256]{3,2,1,0:T(8,128)}, f32[4,64,128]{2,1,0:T(8,128)}) custom-call(f32[19,4,16,256]{3,2,1,0:T(8,128)} %get-tuple-element.14.post, f32[64,128]{1,0:T(8,128)} %copy-done, f32[48,128]{1,0:T(8,128)} %copy-done.3, f32[48,128]{1,0:T(8,128)} %copy-done.4, f32[488,128]{1,0:T(8,128)} %copy-done.1, f32[488,128]{1,0:T(8,128)} %copy-done.2, ...), custom_call_target="tpu_custom_call" | custom-call | tf_op jit(solution)/shard_map/finish/pallas_call | solution.py:399
Async XLA Ops:
  4.6 13.0 %collective-permute-start = (f32[64,128]{1,0:T(8,128)}, f32[64,128]{1,0:T(8,128)S(1)}, u32[]{:S(2)}, u32[]{:S(2)}) collective-permute-start(f32[64,128]{1,0:T(8,128)} %get-tuple-element.15.zbuf), channel_id=1, source_target_pairs={{0,1},{1,0},{2,3},{3,2},{4,5},{5,4},{6,7},{7,6},{8,9},{9,8},{10,11... | collective-permute-start | bytes 98312 | tf_op jit(solution)/shard_map/ppermute | solution.py:378
  17.6 0.6 %copy-start = (f32[64,128]{1,0:T(8,128)}, f32[64,128]{1,0:T(8,128)S(1)}, u32[]{:S(2)}) copy-start(f32[64,128]{1,0:T(8,128)S(1)} %collective-permute-done.zin) | copy-start | bytes 98308
  19.7 7.4 %collective-permute-start.1 = (f32[48,128]{1,0:T(8,128)}, f32[48,128]{1,0:T(8,128)S(1)}, u32[]{:S(2)}, u32[]{:S(2)}) collective-permute-start(f32[48,128]{1,0:T(8,128)} %get-tuple-element.18), channel_id=1, source_target_pairs={{0,2},{2,4},{4,6},{6,8},{8,10},{10,12},{12,14},{14,0},{1,3},{3,5},... | collective-permute-start | bytes 73736 | tf_op jit(solution)/shard_map/ppermute | solution.py:386
  21.6 7.2 %collective-permute-start.2 = (f32[48,128]{1,0:T(8,128)}, f32[48,128]{1,0:T(8,128)S(1)}, u32[]{:S(2)}, u32[]{:S(2)}) collective-permute-start(f32[48,128]{1,0:T(8,128)} %get-tuple-element.19), channel_id=1, source_target_pairs={{0,14},{2,0},{4,2},{6,4},{8,6},{10,8},{12,10},{14,12},{1,15},{3,1}... | collective-permute-start | bytes 73736 | tf_op jit(solution)/shard_map/ppermute | solution.py:387
  27.1 1.7 %copy-start.3 = (f32[48,128]{1,0:T(8,128)}, f32[48,128]{1,0:T(8,128)S(1)}, u32[]{:S(2)}) copy-start(f32[48,128]{1,0:T(8,128)S(1)} %collective-permute-done.1.ypin) | copy-start | bytes 73732
  28.8 0.6 %copy-start.4 = (f32[48,128]{1,0:T(8,128)}, f32[48,128]{1,0:T(8,128)S(1)}, u32[]{:S(2)}) copy-start(f32[48,128]{1,0:T(8,128)S(1)} %collective-permute-done.2.ymin) | copy-start | bytes 73732
  30.8 9.8 %collective-permute-start.3 = (f32[488,128]{1,0:T(8,128)}, f32[488,128]{1,0:T(8,128)S(1)}, u32[]{:S(2)}, u32[]{:S(2)}) collective-permute-start(f32[488,128]{1,0:T(8,128)} %get-tuple-element.23), channel_id=1, source_target_pairs={{0,16},{16,32},{32,48},{48,64},{64,80},{80,96},{96,112},{112,128},... | collective-permute-start | bytes 749576 | tf_op jit(solution)/shard_map/ppermute | solution.py:397
  34.7 11.7 %collective-permute-start.4 = (f32[488,128]{1,0:T(8,128)}, f32[488,128]{1,0:T(8,128)S(1)}, u32[]{:S(2)}, u32[]{:S(2)}) collective-permute-start(f32[488,128]{1,0:T(8,128)} %get-tuple-element.24), channel_id=1, source_target_pairs={{0,496},{16,0},{32,16},{48,32},{64,48},{80,64},{96,80},{112,96},{1... | collective-permute-start | bytes 749576 | tf_op jit(solution)/shard_map/ppermute | solution.py:398
  40.6 5.7 %copy-start.1 = (f32[488,128]{1,0:T(8,128)}, f32[488,128]{1,0:T(8,128)S(1)}, u32[]{:S(2)}) copy-start(f32[488,128]{1,0:T(8,128)S(1)} %collective-permute-done.3.xpin) | copy-start | bytes 749572
  46.3 0.7 %copy-start.2 = (f32[488,128]{1,0:T(8,128)}, f32[488,128]{1,0:T(8,128)S(1)}, u32[]{:S(2)}) copy-start(f32[488,128]{1,0:T(8,128)S(1)} %collective-permute-done.4.xmin) | copy-start | bytes 749572

commit v2 on v1

v2 whole, which is shorter than its diff:
```python
import jax
import jax.numpy as jnp
from jax import lax
from jax.experimental import pallas as pl
from jax.experimental.pallas import tpu as pltpu
from jax.sharding import PartitionSpec as P

F32 = jnp.float32
JET_SPEED = 0.1
H_BASE = 0.5
H_GAIN = 40.0
SHEAR_RATE = 1.6
ODD_RATE = 1.2
EVEN_RATE = 1.4
VEL = (
    (0, 0, 0),
    (1, 0, 0), (-1, 0, 0), (0, 1, 0), (0, -1, 0), (0, 0, 1), (0, 0, -1),
    (1, 1, 0), (-1, -1, 0), (1, -1, 0), (-1, 1, 0),
    (1, 0, 1), (-1, 0, -1), (1, 0, -1), (-1, 0, 1),
    (0, 1, 1), (0, -1, -1), (0, 1, -1), (0, -1, 1),
)
OPP = tuple(VEL.index(tuple(-e for e in v)) for v in VEL)
WEIGHT = (1.0 / 3.0,) + (1.0 / 18.0,) * 6 + (1.0 / 36.0,) * 12
X_UP, X_DN = (1, 7, 9, 11, 13), (2, 10, 8, 14, 12)
Y_UP, Y_DN = (3, 7, 10, 15, 17), (4, 9, 8, 18, 16)
Z_UP, Z_DN = (5, 11, 14, 15, 18), (6, 13, 12, 17, 16)
SX, SZ_, HALF = 4, 16, 128
DEPTH = 64
Z_S, Z_E, Z_ROWS = 40, 56, 64
Y_S, Y_E, Y_D, Y_ROWS = 16, 32, 40, 48
X_U, X_T, X_R, X_ROWS = 160, 416, 432, 440


def roll(value, shift, axis):
    size = value.shape[axis]
    shift = shift % size
    return value if shift == 0 else pltpu.roll(value, shift, axis)


def lanes(shape):
    return lax.broadcasted_iota(jnp.int32, shape, len(shape) - 1)


def rows_of(shape):
    return lax.broadcasted_iota(jnp.int32, shape, 0)


def collide(f):
    s = {i: f[i] + f[i + 1] for i in range(1, 19, 2)}
    d = {i: f[i] - f[i + 1] for i in range(1, 19, 2)}
    s_ab, s_ac, s_bc = s[7] + s[9], s[11] + s[13], s[15] + s[17]
    rho = (f[0] + s[1]) + (s[3] + s[5]) + (s_ab + s_ac + s_bc)
    m_a = d[1] + (d[7] + d[9]) + (d[11] + d[13])
    m_b = d[3] + (d[7] - d[9]) + (d[15] + d[17])
    m_c = d[5] + (d[11] - d[13]) + (d[15] - d[17])
    inv = 1.0 / rho
    u_a, u_b, u_c = m_a * inv, m_b * inv, m_c * inv
    p_aa, p_bb, p_cc = m_a * u_a, m_b * u_b, m_c * u_c
    p_ab, p_ac, p_bc = m_a * u_b, m_a * u_c, m_b * u_c
    q = p_aa + p_bb + p_cc
    base = rho - 1.5 * q
    t = rho - 2.0 * q
    t_ab = 4.0 * f[0] - 2.0 * (s[1] + s[3]) + s_ab - (t + 0.5 * p_cc)
    t_ac = 4.0 * f[0] - 2.0 * (s[1] + s[5]) + s_ac - (t + 0.5 * p_bb)
    t_bc = 4.0 * f[0] - 2.0 * (s[3] + s[5]) + s_bc - (t + 0.5 * p_aa)
    mean = (2.0 / 7.0) * (t_ab + t_ac + t_bc)
    gain = (SHEAR_RATE - EVEN_RATE) / 12.0
    c_ab, c_ac, c_bc = gain * (t_ab - mean), gain * (t_ac - mean), gain * (t_bc - mean)
    keep, half_keep, half = 1.0 - SHEAR_RATE, 0.5 * (1.0 - SHEAR_RATE), 0.5 * SHEAR_RATE
    odd, pull = 0.5 * (1.0 - ODD_RATE), 3.0 * ODD_RATE
    post = [None] * 19
    post[0] = keep * f[0] + (SHEAR_RATE / 3.0) * base + 4.0 * (c_ab + c_ac + c_bc)

    def put(i, extra, equil, moment, weight):
        even = half_keep * s[i] + equil + extra
        anti = odd * d[i] + (pull * weight) * moment
        post[i] = even + anti
        post[i + 1] = even - anti

    axis = half / 9.0
    for i, p, c, m in ((1, p_aa, c_ab + c_ac, m_a), (3, p_bb, c_ab + c_bc, m_b), (5, p_cc, c_ac + c_bc, m_c)):
        put(i, -2.0 * c, axis * (base + 4.5 * p), m, 1.0 / 18.0)
    diag = half / 18.0
    for i, pp, pq, c, m, n in (
        (7, p_aa + p_bb, p_ab, c_ab, m_a, m_b),
        (11, p_aa + p_cc, p_ac, c_ac, m_a, m_c),
        (15, p_bb + p_cc, p_bc, c_bc, m_b, m_c),
    ):
        even = diag * (base + 4.5 * pp)
        cross = (9.0 * diag) * pq
        put(i, c, even + cross, m + n, 1.0 / 36.0)
        put(i + 2, c, even - cross, m - n, 1.0 / 36.0)
    return post, q * inv


def face_kernel(pops, temp, cond, load, cool, zbuf, own, misc, tempv, condv, buf, sems):
    low = lax.axis_index("gz") == 0
    face = jnp.where(low, SZ_ - 1, 0)
    fields = [
        pltpu.make_async_copy(temp, tempv, sems.at[0]),
        pltpu.make_async_copy(cond, condv, sems.at[1]),
        pltpu.make_async_copy(load, misc.at[0:4], sems.at[2]),
        pltpu.make_async_copy(cool, misc.at[4:8], sems.at[3]),
    ]
    rows = []
    for k, layer in enumerate((face, 0)):
        for h in range(2):
            rows.append(pltpu.make_async_copy(
                pops.at[:, :, layer, HALF * h : HALF * h + HALF],
                buf.at[k, :, 4 * h : 4 * h + 4, :],
                sems.at[4 + 2 * k + h],
            ))
    for copy in rows + fields:
        copy.start()
    for copy in fields:
        copy.wait()
    lane = lanes((DEPTH, HALF))
    edges = jnp.zeros((DEPTH, HALF), F32)
    for k, field in enumerate((tempv, condv)):
        for x in range(SX):
            at = k * 16 + x * 4
            edges = jnp.where((lane >= at) & (lane < at + 4), roll(field[x], at + 2, 1), edges)
    own[...] = edges
    lane16 = lanes((16, HALF))
    fold = edges[0:16]
    for g in range(1, 4):
        fold = jnp.where(lane16 >= 32 * g, roll(edges[16 * g : 16 * g + 16], 32 * g, 1), fold)
    zbuf[Z_S : Z_S + 16, :] = fold
    for copy in rows:
        copy.wait()
    out, _ = collide([buf[0, v] for v in range(19)])
    for n in range(5):
        leaving = jnp.where(low, out[Z_UP[n]], out[Z_DN[n]])
        for h in range(2):
            zbuf[20 * h + 4 * n : 20 * h + 4 * n + 4, :] = leaving[4 * h : 4 * h + 4, :]
    _, speed = collide([buf[1, v] for v in range(19)])
    warm = H_BASE + H_GAIN * speed
    misc[8:16, :] = warm
    lane1 = lanes((1, HALF))
    row = jnp.zeros((1, HALF), F32)
    for k in range(4):
        for x in range(SX):
            at = k * 16 + x * 4
            value = misc[4 * k + x : 4 * k + x + 1, :]
            row = jnp.where((lane1 >= at) & (lane1 < at + 2), roll(value, at + 1, 1), row)
    zbuf[Z_E : Z_E + 4, :] = misc[12:16, :]
    zbuf[Z_E + 4 : Z_E + 5, :] = row
    zbuf[Z_E + 5 : Z_E + 8, :] = jnp.zeros((3, HALF), F32)


def collide_kernel(pops, nozzle, wall, tempv, condv, post, yp, ym, xp, xm, nozzlev, wallv, buf, sems):
    copies = [pltpu.make_async_copy(pops.at[:, x], buf.at[:, x], sems.at[x]) for x in range(SX)]
    plates = [
        pltpu.make_async_copy(nozzle, nozzlev, sems.at[SX]),
        pltpu.make_async_copy(wall, wallv, sems.at[SX + 1]),
    ]
    for copy in copies + plates:
        copy.start()
    for k, field in enumerate((tempv, condv)):
        for buffer, near, far in ((xp, 3, 2), (xm, 0, 1)):
            at = X_U + 128 * k
            buffer[at : at + 64, :] = field[near]
            buffer[at + 64 : at + 128, :] = field[far]
    y_up = [jnp.zeros((8, HALF), F32) for _ in range(2)]
    y_dn = [jnp.zeros((8, HALF), F32) for _ in range(2)]
    lane8 = lanes((8, HALF))
    for x in range(SX):
        copies[x].wait()
        for k in range(2):
            z = slice(8 * k, 8 * k + 8)
            for h in range(2):
                y = slice(HALF * h, HALF * h + HALF)
                out, _ = collide([buf[v, x, z, y] for v in range(19)])
                for v in range(19):
                    post[v, x, z, y] = out[v]
                for n in range(5):
                    at = 4 * n + x
                    if h == 1:
                        y_up[k] = jnp.where(lane8 == at, roll(out[Y_UP[n]], at - 127, 1), y_up[k])
                    else:
                        y_dn[k] = jnp.where(lane8 == at, roll(out[Y_DN[n]], at, 1), y_dn[k])
                    at = 32 * n + 16 * h + 8 * k
                    if x == 3:
                        xp[at : at + 8, :] = out[X_UP[n]]
                    if x == 0:
                        xm[at : at + 8, :] = out[X_DN[n]]
    for k in range(2):
        yp[8 * k : 8 * k + 8, :] = y_up[k]
        ym[8 * k : 8 * k + 8, :] = y_dn[k]
    for copy in plates:
        copy.wait()


def y_kernel(yp, ym, zbuf, zin, outp, outm):
    low = lax.axis_index("gz") == 0
    lane = lanes((1, HALF))
    sent = zin[Z_E + 4 : Z_E + 5, :]
    row = jnp.where((lane >= 32) & low, zbuf[Z_E + 4 : Z_E + 5, :], sent)
    for out, edge, first in ((outp, yp, 20 + 12), (outm, ym, 16)):
        out[0:16, :] = edge[...]
        out[Y_S : Y_S + 16, :] = zin[Z_S : Z_S + 16, :]
        out[Y_E : Y_E + 8, :] = jnp.broadcast_to(row, (8, HALF))
        out[Y_D : Y_D + 4, :] = zin[first : first + 4, :]
        out[Y_D + 4 : Y_D + 8, :] = jnp.zeros((4, HALF), F32)


def halo_slabs(low, zin, ypin, ymin):
    left = jnp.where(low, ypin[Y_S : Y_S + 16, :], zin[Z_S : Z_S + 16, :])
    right = jnp.where(low, zin[Z_S : Z_S + 16, :], ymin[Y_S : Y_S + 16, :])
    return left, right


def x_kernel(inp, inm, zin, ypin, ymin, misc, outp, outm):
    low = lax.axis_index("gz") == 0
    left, right = halo_slabs(low, zin, ypin, ymin)
    warm = jnp.where(low, misc[8:12, :], zin[Z_E : Z_E + 4, :])
    lane = lanes((16, HALF))
    for out, x, n, up, dn in ((outp, 3, 1, 7, 9), (outm, 0, 2, 10, 8)):
        k_up, k_dn = 4 * Y_UP.index(up) + x, 4 * Y_DN.index(dn) + x + 1
        slab = jnp.where((lane & 15) == 4 * x + 1, left, right)
        slab = jnp.where(lane == k_up, ypin[0:16, :], slab)
        out[X_T : X_T + 16, :] = jnp.where(lane == k_dn, roll(ymin[0:16, :], 1, 1), slab)
        for h in range(2):
            row = 20 * h + 4 * n + x
            out[X_R + h : X_R + h + 1, :] = zin[row : row + 1, :]
        out[X_R + 2 : X_R + 3, :] = misc[x : x + 1, :]
        out[X_R + 3 : X_R + 4, :] = misc[4 + x : 5 + x, :]
        out[X_R + 4 : X_R + 5, :] = warm[x : x + 1, :]
        out[X_R + 5 : X_R + 8, :] = jnp.zeros((3, HALF), F32)


def stream(v, x, low, post, zin, ypin, ymin, xpin, xmin, nozzle, wall):
    lane = lanes((SZ_, HALF))
    layer = rows_of((SZ_, HALF))
    a, b, c = VEL[v]
    s = x - a
    inside = 0 <= s < SX
    edge = xpin if s < 0 else xmin
    if inside:
        tiles = [post[v, s, :, HALF * h : HALF * h + HALF] for h in range(2)]
    else:
        n = (X_UP if s < 0 else X_DN).index(v)
        tiles = [edge[32 * n + 16 * h : 32 * n + 16 * h + 16, :] for h in range(2)]
    beside = None
    if b:
        slab = ypin if b > 0 else ymin
        k = 4 * (Y_UP if b > 0 else Y_DN).index(v)
        if inside:
            k, column = k + s, slab[0:16, :]
        else:
            k, column = k + (3 if s < 0 else 0) + (1 if b < 0 else 0), edge[X_T : X_T + 16, :]
        beside = roll(column, (0 if b > 0 else HALF - 1) - k, 1)
    if c:
        n = (Z_UP if c > 0 else Z_DN).index(v)
        at = 0 if c > 0 else SZ_ - 1
        for h in range(2):
            k = 20 * h + 4 * n + s
            row = zin[k : k + 1, :] if inside else edge[X_R + h : X_R + h + 1, :]
            tiles[h] = jnp.where(layer == at, row, roll(tiles[h], c, 0))
        if b:
            corner = roll(slab[Y_D + x : Y_D + x + 1, :], b, 1)
            beside = jnp.where(layer == at, corner, roll(beside, c, 0))
    if b > 0:
        t0, t1 = roll(tiles[0], 1, 1), roll(tiles[1], 1, 1)
        tiles = [jnp.where(lane == 0, beside, t0), jnp.where(lane == 0, t0, t1)]
    elif b < 0:
        t0, t1 = roll(tiles[0], -1, 1), roll(tiles[1], -1, 1)
        tiles = [jnp.where(lane == HALF - 1, t1, t0), jnp.where(lane == HALF - 1, beside, t1)]
    for h in range(2):
        y = slice(HALF * h, HALF * h + HALF)
        if c > 0:
            back = post[OPP[v], x, 0:1, y]
            tiles[h] = jnp.where((layer == 0) & low, back, tiles[h])
        elif c < 0:
            back = post[OPP[v], x, SZ_ - 1 : SZ_, y]
            through = post[v, x, SZ_ - 1 : SZ_, y]
            top = jnp.where(
                nozzle[x : x + 1, y] == 1,
                back + 6.0 * WEIGHT[v] * JET_SPEED,
                jnp.where(wall[x : x + 1, y] == 1, through, back),
            )
            tiles[h] = jnp.where((layer == SZ_ - 1) & jnp.logical_not(low), top, tiles[h])
    return tiles


INNER = tuple(v for v in range(19) if VEL[v][1] == 0)
SIDE = tuple(v for v in range(19) if VEL[v][1] != 0)


def put_inside(velocities, low, out, buf, sems, *state):
    copies = []
    for i, v in enumerate(velocities):
        a = VEL[v][0]
        first, last = max(a, 0), SX + min(a, 0)
        for x in range(first, last):
            for h, tile in enumerate(stream(v, x, low, *state)):
                buf[i, x, :, HALF * h : HALF * h + HALF] = tile
        copy = pltpu.make_async_copy(buf.at[i, first:last], out.at[v, first:last], sems.at[i])
        copy.start()
        copies.append(copy)
    for copy in copies:
        copy.wait()


def inner_kernel(post, zin, nozzle, wall, out, buf, sems):
    low = lax.axis_index("gz") == 0
    put_inside(INNER, low, out, buf, sems, post, zin, None, None, None, None, nozzle, wall)


def side_kernel(whole, post, zin, ypin, ymin, nozzle, wall, out, buf, sems):
    low = lax.axis_index("gz") == 0
    put_inside(SIDE, low, out, buf, sems, post, zin, ypin, ymin, None, None, nozzle, wall)


def final_kernel(
    whole, post, zin, ypin, ymin, xpin, xmin, nozzle, wall, temp, cond, own, misc, zbuf,
    pops_out, solid_out, buf, solid, sems,
):
    low = lax.axis_index("gz") == 0
    copies = []
    for i, v in enumerate(X_UP + X_DN):
        x = 0 if i < 5 else SX - 1
        for h, tile in enumerate(stream(v, x, low, post, zin, ypin, ymin, xpin, xmin, nozzle, wall)):
            buf[i, :, HALF * h : HALF * h + HALF] = tile
        copies.append(pltpu.make_async_copy(buf.at[i], pops_out.at[v, x], sems.at[i]))
        copies[-1].start()

    lane = lanes((DEPTH, HALF))
    depth = rows_of((DEPTH, HALF))
    floor, face = depth == 0, depth == DEPTH - 1

    def spread(folded, at):
        return jnp.concatenate([roll(folded, at - 32 * g, 1) for g in range(4)], axis=0)

    def vertical(c):
        down = jnp.where(face, 0.0, 0.5 * (c + roll(c, -1, 0)))
        return down, roll(down, 1, 0)

    def around(links):
        total = None
        for link, value in links:
            total = link * value if total is None else total + link * value
        return total

    U = {x: temp[x] for x in range(SX)}
    C = {x: cond[x] for x in range(SX)}
    for near, far, edge in ((-1, -2, xpin), (4, 5, xmin)):
        U[near], U[far] = edge[X_U : X_U + 64, :], edge[X_U + 64 : X_U + 128, :]
        C[near], C[far] = edge[X_U + 128 : X_U + 192, :], edge[X_U + 192 : X_U + 256, :]
    warm = jnp.where(low, misc[8:12, :], zin[Z_E : Z_E + 4, :])
    loads = {x: misc[x : x + 1, :] for x in range(SX)}
    cools = {x: misc[4 + x : 5 + x, :] for x in range(SX)}
    warms = {x: warm[x : x + 1, :] for x in range(SX)}
    for x, edge in ((-1, xpin), (4, xmin)):
        loads[x], cools[x], warms[x] = (edge[X_R + 2 + k : X_R + 3 + k, :] for k in range(3))

    left, right = halo_slabs(low, zin, ypin, ymin)
    own_edges = own[...]
    near_first = {}
    side = {}
    row_left = jnp.where(low, ypin[Y_E : Y_E + 1, :], zin[Z_E + 4 : Z_E + 5, :])
    row_right = jnp.where(low, zin[Z_E + 4 : Z_E + 5, :], ymin[Y_E : Y_E + 1, :])
    heat_left = jnp.where(low, roll(row_left, -48, 1), roll(row_left, -32, 1))
    heat_right = jnp.where(low, roll(zbuf[Z_E + 4 : Z_E + 5, :], -49, 1), roll(row_right, -33, 1))
    before, after = xpin[X_T : X_T + 16, :], xmin[X_T : X_T + 16, :]
    for name, folded, j1, j2, jo, row, h_row, jr in (
        ("left", left, 1, 0, 2, row_left, heat_left, 0),
        ("right", right, 2, 3, 1, row_right, heat_right, 1),
    ):
        u1, u2 = spread(folded, -j1), spread(folded, -j2)
        c1, c2 = spread(folded, -16 - j1), spread(folded, -16 - j2)
        u1 = jnp.where(lane == 124, spread(before, 124 - 12 - j1), jnp.where(lane == 16, spread(after, 16 - j1), u1))
        c1 = jnp.where(lane == 124, spread(before, 124 - 28 - j1), jnp.where(lane == 16, spread(after, -j1), c1))
        side[name] = (u1, c1)
        uo, co = roll(own_edges, -jo, 1), roll(own_edges, -16 - jo, 1)
        g_far, g_own = 0.5 * (c1 + c2), 0.5 * (c1 + co)
        g_up = 0.5 * (c1 + roll(c1, -4, 1))
        g_dn = roll(g_up, 4, 1)
        v_dn, v_up = vertical(c1)
        e_load, e_cool = roll(row, -jr, 1), roll(row, -16 - jr, 1)
        num = u1 + jnp.where(floor, e_load, 0.0) + jnp.where(face, h_row * e_cool, 0.0)
        den = 1.0 + jnp.where(face, h_row, 0.0) + (g_far + g_own) + (g_up + g_dn) + (v_dn + v_up)
        num = num + around(((g_far, u2), (g_own, uo), (g_up, roll(u1, -4, 1)), (g_dn, roll(u1, 4, 1)),
                            (v_dn, roll(u1, -1, 0)), (v_up, roll(u1, 1, 0))))
        near_first[name] = num / den

    def beside_of(value, left_col, right_col):
        return (
            jnp.where(lane == 0, left_col, roll(value, 1, 1)),
            jnp.where(lane == HALF - 1, right_col, roll(value, -1, 1)),
        )

    def columns(pair, x):
        at = (4 * x) % HALF
        return roll(pair[0], -at, 1), roll(pair[1], HALF - 1 - at, 1)

    pair_u = (side["left"][0], side["right"][0])
    pair_c = (side["left"][1], side["right"][1])
    pair_f = (near_first["left"], near_first["right"])
    g_x = {x: 0.5 * (C[x] + C[x + 1]) for x in range(-2, 5)}
    first, kept = {}, {}
    for x in range(-1, 5):
        c_l, c_r = beside_of(C[x], *columns(pair_c, x))
        u_l, u_r = beside_of(U[x], *columns(pair_u, x))
        g_l, g_r = 0.5 * (C[x] + c_l), 0.5 * (C[x] + c_r)
        v_dn, v_up = vertical(C[x])
        base = U[x] + jnp.where(floor, loads[x], 0.0) + jnp.where(face, warms[x] * cools[x], 0.0)
        den = 1.0 + jnp.where(face, warms[x], 0.0) + (g_x[x - 1] + g_x[x]) + (g_l + g_r) + (v_dn + v_up)
        inv = 1.0 / den
        num = base + around(((g_x[x - 1], U[x - 1]), (g_x[x], U[x + 1]), (g_l, u_l), (g_r, u_r),
                             (v_dn, roll(U[x], -1, 0)), (v_up, roll(U[x], 1, 0))))
        first[x] = num * inv
        kept[x] = (base, inv, g_l, g_r, v_dn, v_up)
    for x in range(SX):
        base, inv, g_l, g_r, v_dn, v_up = kept[x]
        f_l, f_r = beside_of(first[x], *columns(pair_f, x))
        num = base + around(((g_x[x - 1], first[x - 1]), (g_x[x], first[x + 1]), (g_l, f_l), (g_r, f_r),
                             (v_dn, roll(first[x], -1, 0)), (v_up, roll(first[x], 1, 0))))
        solid[x] = num * inv
        copies.append(pltpu.make_async_copy(solid.at[x], solid_out.at[x], sems.at[10 + x]))
        copies[-1].start()
    for copy in copies:
        copy.wait()


def shape(*dims):
    return jax.ShapeDtypeStruct(dims, F32)


def near(*dims):
    return pltpu.VMEM(dims, F32)


def hold(*arrays):
    return [pltpu.with_memory_space_constraint(a, pltpu.VMEM) for a in arrays]


VM = pl.BlockSpec(memory_space=pltpu.VMEM)
ANY = pl.BlockSpec(memory_space=pl.ANY)


def ring(axis, step):
    n = lax.axis_size(axis)
    return [(i, (i + step) % n) for i in range(n)]


def call(kernel, name, inputs, outputs, scratch=(), aliases=None):
    spaces = [ANY if kind == "far" else VM for kind, _ in inputs]
    arrays = [hold(a)[0] if kind == "near" else a for kind, a in inputs]
    return pl.pallas_call(
        kernel,
        name=name,
        in_specs=spaces,
        out_specs=[ANY if isinstance(o, jax.ShapeDtypeStruct) else VM for o in outputs],
        out_shape=list(outputs),
        scratch_shapes=list(scratch),
        input_output_aliases=aliases or {},
    )(*arrays)


def far(*arrays):
    return [("far", a) for a in arrays]


def kept(*arrays):
    return [("near", a) for a in arrays]


def body(populations, nozzle_mask, wall_type, solid_temp, diffusion, heat_load, coolant_temp):
    dma = pltpu.SemaphoreType.DMA
    zbuf, own, misc, temp, cond = call(
        face_kernel, "face",
        far(populations, solid_temp, diffusion, heat_load, coolant_temp),
        [near(Z_ROWS, HALF), near(DEPTH, HALF), near(16, HALF), near(SX, DEPTH, HALF), near(SX, DEPTH, HALF)],
        [pltpu.VMEM((2, 19, 8, HALF), F32), dma((8,))],
    )
    zin = lax.ppermute(zbuf, "gz", ring("gz", 1))
    post, yp, ym, xp, xm, nozzle, wall = call(
        collide_kernel, "collide",
        far(populations, nozzle_mask, wall_type) + kept(temp, cond),
        [near(19, SX, SZ_, 2 * HALF), near(16, HALF), near(16, HALF), near(X_ROWS, HALF), near(X_ROWS, HALF),
         pltpu.VMEM((SX, 2 * HALF), jnp.int32), pltpu.VMEM((SX, 2 * HALF), jnp.int32)],
        [pltpu.VMEM((19, SX, SZ_, 2 * HALF), F32), dma((SX + 2,))],
    )
    ypo, ymo = call(y_kernel, "pack_y", kept(yp, ym, zbuf, zin), [near(Y_ROWS, HALF)] * 2)
    ypin = lax.ppermute(ypo, "gy", ring("gy", 1))
    ymin = lax.ppermute(ymo, "gy", ring("gy", -1))
    (pops,) = call(
        inner_kernel, "inner", kept(post, zin, nozzle, wall), [shape(19, SX, SZ_, 2 * HALF)],
        [pltpu.VMEM((len(INNER), SX, SZ_, 2 * HALF), F32), dma((len(INNER),))],
    )
    xpo, xmo = call(
        x_kernel, "pack_x", kept(xp, xm, zin, ypin, ymin, misc), [near(X_ROWS, HALF)] * 2, aliases={0: 0, 1: 1}
    )
    xpin = lax.ppermute(xpo, "gx", ring("gx", 1))
    xmin = lax.ppermute(xmo, "gx", ring("gx", -1))
    (pops,) = call(
        side_kernel, "side", far(pops) + kept(post, zin, ypin, ymin, nozzle, wall), [shape(19, SX, SZ_, 2 * HALF)],
        [pltpu.VMEM((len(SIDE), SX, SZ_, 2 * HALF), F32), dma((len(SIDE),))], {0: 0},
    )
    return tuple(call(
        final_kernel, "finish",
        far(pops) + kept(post, zin, ypin, ymin, xpin, xmin, nozzle, wall, temp, cond, own, misc, zbuf),
        [shape(19, SX, SZ_, 2 * HALF), shape(SX, DEPTH, HALF)],
        [pltpu.VMEM((10, SZ_, 2 * HALF), F32), pltpu.VMEM((SX, DEPTH, HALF), F32), dma((14,))], {0: 0},
    ))


def solution(mesh):
    placed = (
        P(None, "gx", "gz", "gy"),
        P("gx", "gy"),
        P("gx", "gy"),
        P("gx", None, ("gy", "gz")),
        P("gx", None, ("gy", "gz")),
        P("gx", ("gy", "gz")),
        P("gx", ("gy", "gz")),
    )
    return jax.shard_map(
        body,
        mesh=mesh,
        in_specs=placed,
        out_specs=(P(None, "gx", "gz", "gy"), P("gx", None, ("gy", "gz"))),
        check_vma=False,
    )
```

time: 51.7 us -> 41.1 us (0.79)
  waiting for transfers between devices: 13.4 us -> 8.83 us
  Pallas kernels: 11 us -> 7.17 us
  local copies, waits for them, and re-layouts: 1.93 us -> 0 us
    pallas_call x4 -> x7, Pallas kernels: 11 us -> 7.17 us  [call(): pl.pallas_call(kernel, name=name, in_specs=spaces, out_specs=[ANY if isin...]
    ppermute x1, waiting for transfers between devices: 3.94 us -> 1.3 us  [body(): xpin = lax.ppermute(xpo, 'gx', ring('gx', 1))]
    ppermute x1, waiting for transfers between devices: 2.12 us -> 0.09 us  [body(): zin = lax.ppermute(zbuf, 'gz', ring('gz', 1))]
    unnamed x10 -> x0, local copies, waits for them, and re-layouts: 1.93 us -> none
  transfers between devices with their start and end apart: 5 -> 5, of which waited for: 4 -> 4; matrix products, arithmetic and copies ran while one was open for 0% -> 0% of each run, Pallas kernels for 0% -> 9%
where the time goes in v2:
time: 41.1 us; the launch traced here: 40.8 us
  starting transfers between devices  24.1 us (59%)
  waiting for transfers between devices  8.83 us (21%)
  Pallas kernels  7.17 us (17%)
  between operations  0.72 us (2%)
    ppermute x1, starting transfers between devices, body(): zin = lax.ppermute(zbuf, 'gz', ring('gz', 1))  10.9 us
    pallas_call x7, Pallas kernels, call(): pl.pallas_call(kernel, name=name, in_specs=spaces, out_specs=[ANY if isin...  7.17 us
    ppermute x1, waiting for transfers between devices, body(): xmin = lax.ppermute(xmo, 'gx', ring('gx', -1))  5.96 us
    ppermute x1, starting transfers between devices, body(): ymin = lax.ppermute(ymo, 'gy', ring('gy', -1))  5.44 us
    ppermute x1, starting transfers between devices, body(): xpin = lax.ppermute(xpo, 'gx', ring('gx', 1))  3.81 us
    ppermute x1, starting transfers between devices, body(): xmin = lax.ppermute(xmo, 'gx', ring('gx', -1))  2.02 us
    ppermute x1, starting transfers between devices, body(): ypin = lax.ppermute(ypo, 'gy', ring('gy', 1))  1.92 us
    ppermute x1, waiting for transfers between devices, body(): ymin = lax.ppermute(ymo, 'gy', ring('gy', -1))  1.49 us
  transfers between devices with their start and end apart: 5, of which 4 were waited for; matrix products, arithmetic and copies ran while one was open for 0% of the time, Pallas kernels for 9%

profile of v2, /device:TPU:62, one launch (start us, length us, event | category | flops | bytes accessed | tf_op | source)
XLA Modules:
  0.0 40.8 jit_solution(523457789434201987)
XLA Ops:
  0.6 1.5 %face.1 = (f32[64,128]{1,0:T(8,128)S(1)}, f32[64,128]{1,0:T(8,128)S(1)}, f32[16,128]{1,0:T(8,128)S(1)}, f32[4,64,128]{2,1,0:T(8,128)S(1)}, f32[4,64,128]{2,1,0:T(8,128)S(1)}) custom-call(f32[19,4,16,256]{3,2,1,0:T(8,128)} %pops.3, f32[4,64,128]{2,1,0:T(8,128)} %temp.1, f32[4,64,128]{2,1,0:T(8,128)} %cond.1, f32[4,128]{1,0:T(4,128)} %load.1, f32[4,128]{1,0:T(4,128)} %cool.1), custom_call_target="tpu_custom_call" | custom-call | tf_op jit(solution)/shard_map/face/pallas_call | solution.py:450
  2.1 10.9 %collective-permute-start = (f32[64,128]{1,0:T(8,128)S(1)}, f32[64,128]{1,0:T(8,128)S(1)}, u32[]{:S(2)}, u32[]{:S(2)}) collective-permute-start(f32[64,128]{1,0:T(8,128)S(1)} %get-tuple-element.21.zbuf), channel_id=1, source_target_pairs={{0,1},{1,0},{2,3},{3,2},{4,5},{5,4},{6,7},{7,6},{8,9},{9,8},{10,11... | collective-permute-start | bytes 98312 | tf_op jit(solution)/shard_map/ppermute | solution.py:477
  13.0 1.8 %collide.1 = (f32[19,4,16,256]{3,2,1,0:T(8,128)S(1)}, f32[16,128]{1,0:T(8,128)S(1)}, f32[16,128]{1,0:T(8,128)S(1)}, f32[440,128]{1,0:T(8,128)S(1)}, f32[440,128]...) custom-call(f32[19,4,16,256]{3,2,1,0:T(8,128)} %pops.3, s32[4,256]{1,0:T(4,128)} %nozzle.1, s32[4,256]{1,0:T(4,128)} %wall.1, ...), custom_call_target="tpu_custom_call" | custom-call | tf_op jit(solution)/shard_map/collide/pallas_call | solution.py:450
  14.9 0.1 collective-permute-done.zin
  15.0 1.9 %collective-permute-start.1 = (f32[48,128]{1,0:T(8,128)S(1)}, f32[48,128]{1,0:T(8,128)S(1)}, u32[]{:S(2)}, u32[]{:S(2)}) collective-permute-start(f32[48,128]{1,0:T(8,128)S(1)} %get-tuple-element.26), channel_id=1, source_target_pairs={{0,2},{2,4},{4,6},{6,8},{8,10},{10,12},{12,14},{14,0},{1,3},{3,5},... | collective-permute-start | bytes 73736 | tf_op jit(solution)/shard_map/ppermute | solution.py:486
  16.9 5.4 %collective-permute-start.2 = (f32[48,128]{1,0:T(8,128)S(1)}, f32[48,128]{1,0:T(8,128)S(1)}, u32[]{:S(2)}, u32[]{:S(2)}) collective-permute-start(f32[48,128]{1,0:T(8,128)S(1)} %get-tuple-element.27), channel_id=1, source_target_pairs={{0,14},{2,0},{4,2},{6,4},{8,6},{10,8},{12,10},{14,12},{1,15},{3,1}... | collective-permute-start | bytes 73736 | tf_op jit(solution)/shard_map/ppermute | solution.py:487
  22.3 0.0 collective-permute-done.1.ypin
  22.3 1.5 %collective-permute-done.2.ymin = f32[48,128]{1,0:T(8,128)S(1)} collective-permute-done((f32[48,128]{1,0:T(8,128)S(1)}, f32[48,128]{1,0:T(8,128)S(1)}, u32[]{:S(2)}, u32[]{:S(2)}) %collective-permute-start.2) | collective-permute-done | bytes 24608 | tf_op jit(solution)/shard_map/ppermute | solution.py:487
  23.8 0.1 pack_x.1
  23.9 3.8 %collective-permute-start.3 = (f32[440,128]{1,0:T(8,128)S(1)}, f32[440,128]{1,0:T(8,128)S(1)}, u32[]{:S(2)}, u32[]{:S(2)}) collective-permute-start(f32[440,128]{1,0:T(8,128)S(1)} %get-tuple-element.31), channel_id=1, source_target_pairs={{0,16},{16,32},{32,48},{48,64},{64,80},{80,96},{96,112},{112,128},... | collective-permute-start | bytes 675848 | tf_op jit(solution)/shard_map/ppermute | solution.py:495
  27.7 2.0 %collective-permute-start.4 = (f32[440,128]{1,0:T(8,128)S(1)}, f32[440,128]{1,0:T(8,128)S(1)}, u32[]{:S(2)}, u32[]{:S(2)}) collective-permute-start(f32[440,128]{1,0:T(8,128)S(1)} %get-tuple-element.32), channel_id=1, source_target_pairs={{0,496},{16,0},{32,16},{48,32},{64,48},{80,64},{96,80},{112,96},{1... | collective-permute-start | bytes 675848 | tf_op jit(solution)/shard_map/ppermute | solution.py:496
  29.7 0.8 %inner.1.whole = f32[19,4,16,256]{3,2,1,0:T(8,128)} custom-call(f32[19,4,16,256]{3,2,1,0:T(8,128)S(1)} %get-tuple-element.20.post, f32[64,128]{1,0:T(8,128)S(1)} %collective-permute-done.zin, s32[4,256]{1,0:T(4,128)S(1)} %get-tuple-element.22.nozzle, s32[4,256]{1,0:T(4,128)S(1)} %get-tuple-element.23.wall), custom_call_target="tpu_custom_call" | custom-call | tf_op jit(solution)/shard_map/inner/pallas_call | solution.py:450
  30.6 1.0 %side.1.whole = f32[19,4,16,256]{3,2,1,0:T(8,128)} custom-call(f32[19,4,16,256]{3,2,1,0:T(8,128)} %inner.1.whole, f32[19,4,16,256]{3,2,1,0:T(8,128)S(1)} %get-tuple-element.20.post, f32[64,128]{1,0:T(8,128)S(1)} %collective-permute-done.zin, f32[48,128]{1,0:T(8,128)S(1)} %collective-permute-done.1.ypin, ...), custom_call_target="tpu_custom_call", output_to_operand_aliasing={{}: (0, {})} | custom-call | tf_op jit(solution)/shard_map/side/pallas_call | solution.py:450
  31.7 1.3 %collective-permute-done.3.xpin = f32[440,128]{1,0:T(8,128)S(1)} collective-permute-done((f32[440,128]{1,0:T(8,128)S(1)}, f32[440,128]{1,0:T(8,128)S(1)}, u32[]{:S(2)}, u32[]{:S(2)}) %collective-permute-start.3) | collective-permute-done | bytes 225312 | tf_op jit(solution)/shard_map/ppermute | solution.py:495
  32.9 6.0 %collective-permute-done.4.xmin = f32[440,128]{1,0:T(8,128)S(1)} collective-permute-done((f32[440,128]{1,0:T(8,128)S(1)}, f32[440,128]{1,0:T(8,128)S(1)}, u32[]{:S(2)}, u32[]{:S(2)}) %collective-permute-start.4) | collective-permute-done | bytes 225312 | tf_op jit(solution)/shard_map/ppermute | solution.py:496
  38.9 1.9 %finish.1 = (f32[19,4,16,256]{3,2,1,0:T(8,128)}, f32[4,64,128]{2,1,0:T(8,128)}) custom-call(f32[19,4,16,256]{3,2,1,0:T(8,128)} %side.1.whole, f32[19,4,16,256]{3,2,1,0:T(8,128)S(1)} %get-tuple-element.20.post, f32[64,128]{1,0:T(8,128)S(1)} %collective-permute-done.zin, f32[48,128]{1,0:T(8,128)S(1)} %collective-permute-done.1.ypin, ...), custom_call_target="tpu_custom_call", output_to_operand_aliasing={{0}: (0, {})} | custom-call | tf_op jit(solution)/shard_map/finish/pallas_call | solution.py:450
  (1 shorter events, 0.0 us)
Async XLA Ops:
  2.1 12.8 %collective-permute-start = (f32[64,128]{1,0:T(8,128)S(1)}, f32[64,128]{1,0:T(8,128)S(1)}, u32[]{:S(2)}, u32[]{:S(2)}) collective-permute-start(f32[64,128]{1,0:T(8,128)S(1)} %get-tuple-element.21.zbuf), channel_id=1, source_target_pairs={{0,1},{1,0},{2,3},{3,2},{4,5},{5,4},{6,7},{7,6},{8,9},{9,8},{10,11... | collective-permute-start | bytes 98312 | tf_op jit(solution)/shard_map/ppermute | solution.py:477
  15.0 7.4 %collective-permute-start.1 = (f32[48,128]{1,0:T(8,128)S(1)}, f32[48,128]{1,0:T(8,128)S(1)}, u32[]{:S(2)}, u32[]{:S(2)}) collective-permute-start(f32[48,128]{1,0:T(8,128)S(1)} %get-tuple-element.26), channel_id=1, source_target_pairs={{0,2},{2,4},{4,6},{6,8},{8,10},{10,12},{12,14},{14,0},{1,3},{3,5},... | collective-permute-start | bytes 73736 | tf_op jit(solution)/shard_map/ppermute | solution.py:486
  16.9 6.9 %collective-permute-start.2 = (f32[48,128]{1,0:T(8,128)S(1)}, f32[48,128]{1,0:T(8,128)S(1)}, u32[]{:S(2)}, u32[]{:S(2)}) collective-permute-start(f32[48,128]{1,0:T(8,128)S(1)} %get-tuple-element.27), channel_id=1, source_target_pairs={{0,14},{2,0},{4,2},{6,4},{8,6},{10,8},{12,10},{14,12},{1,15},{3,1}... | collective-permute-start | bytes 73736 | tf_op jit(solution)/shard_map/ppermute | solution.py:487
  23.9 9.0 %collective-permute-start.3 = (f32[440,128]{1,0:T(8,128)S(1)}, f32[440,128]{1,0:T(8,128)S(1)}, u32[]{:S(2)}, u32[]{:S(2)}) collective-permute-start(f32[440,128]{1,0:T(8,128)S(1)} %get-tuple-element.31), channel_id=1, source_target_pairs={{0,16},{16,32},{32,48},{48,64},{64,80},{80,96},{96,112},{112,128},... | collective-permute-start | bytes 675848 | tf_op jit(solution)/shard_map/ppermute | solution.py:495
  27.7 11.2 %collective-permute-start.4 = (f32[440,128]{1,0:T(8,128)S(1)}, f32[440,128]{1,0:T(8,128)S(1)}, u32[]{:S(2)}, u32[]{:S(2)}) collective-permute-start(f32[440,128]{1,0:T(8,128)S(1)} %get-tuple-element.32), channel_id=1, source_target_pairs={{0,496},{16,0},{32,16},{48,32},{64,48},{80,64},{96,80},{112,96},{1... | collective-permute-start | bytes 675848 | tf_op jit(solution)/shard_map/ppermute | solution.py:496

commit v3 on v2

--- a/solution.py
+++ b/solution.py
@@ -93,6 +93,10 @@
     return post, q * inv
 
 
+def even(axis):
+    return (lax.axis_index(axis) & 1) == 0
+
+
 def face_kernel(pops, temp, cond, load, cool, zbuf, own, misc, tempv, condv, buf, sems):
     low = lax.axis_index("gz") == 0
     face = jnp.where(low, SZ_ - 1, 0)
@@ -102,16 +106,25 @@
         pltpu.make_async_copy(load, misc.at[0:4], sems.at[2]),
         pltpu.make_async_copy(cool, misc.at[4:8], sems.at[3]),
     ]
-    rows = []
-    for k, layer in enumerate((face, 0)):
-        for h in range(2):
-            rows.append(pltpu.make_async_copy(
+    rows = [
+        [
+            pltpu.make_async_copy(
                 pops.at[:, :, layer, HALF * h : HALF * h + HALF],
                 buf.at[k, :, 4 * h : 4 * h + 4, :],
                 sems.at[4 + 2 * k + h],
-            ))
-    for copy in rows + fields:
+            )
+            for h in range(2)
+        ]
+        for k, layer in enumerate((face, 0))
+    ]
+    for copy in rows[0] + fields:
         copy.start()
+
+    @pl.when(low)
+    def _():
+        for copy in rows[1]:
+            copy.start()
+
     for copy in fields:
         copy.wait()
     lane = lanes((DEPTH, HALF))
@@ -126,16 +139,22 @@
     for g in range(1, 4):
         fold = jnp.where(lane16 >= 32 * g, roll(edges[16 * g : 16 * g + 16], 32 * g, 1), fold)
     zbuf[Z_S : Z_S + 16, :] = fold
-    for copy in rows:
+    for copy in rows[0]:
         copy.wait()
     out, _ = collide([buf[0, v] for v in range(19)])
     for n in range(5):
         leaving = jnp.where(low, out[Z_UP[n]], out[Z_DN[n]])
         for h in range(2):
             zbuf[20 * h + 4 * n : 20 * h + 4 * n + 4, :] = leaving[4 * h : 4 * h + 4, :]
-    _, speed = collide([buf[1, v] for v in range(19)])
-    warm = H_BASE + H_GAIN * speed
-    misc[8:16, :] = warm
+    misc[8:16, :] = jnp.zeros((8, HALF), F32)
+
+    @pl.when(low)
+    def _():
+        for copy in rows[1]:
+            copy.wait()
+        _, speed = collide([buf[1, v] for v in range(19)])
+        misc[8:16, :] = H_BASE + H_GAIN * speed
+
     lane1 = lanes((1, HALF))
     row = jnp.zeros((1, HALF), F32)
     for k in range(4):
@@ -148,7 +167,7 @@
     zbuf[Z_E + 5 : Z_E + 8, :] = jnp.zeros((3, HALF), F32)
 
 
-def collide_kernel(pops, nozzle, wall, tempv, condv, post, yp, ym, xp, xm, nozzlev, wallv, buf, sems):
+def collide_kernel(pops, nozzle, wall, tempv, condv, post, yp, ym, xa, xb, nozzlev, wallv, buf, face, sems):
     copies = [pltpu.make_async_copy(pops.at[:, x], buf.at[:, x], sems.at[x]) for x in range(SX)]
     plates = [
         pltpu.make_async_copy(nozzle, nozzlev, sems.at[SX]),
@@ -156,11 +175,13 @@
     ]
     for copy in copies + plates:
         copy.start()
+    paired = even("gx")
     for k, field in enumerate((tempv, condv)):
-        for buffer, near, far in ((xp, 3, 2), (xm, 0, 1)):
-            at = X_U + 128 * k
-            buffer[at : at + 64, :] = field[near]
-            buffer[at + 64 : at + 128, :] = field[far]
+        for j in range(2):
+            at = X_U + 128 * k + 64 * j
+            up, dn = field[3 - j], field[j]
+            xa[at : at + 64, :] = jnp.where(paired, up, dn)
+            xb[at : at + 64, :] = jnp.where(paired, dn, up)
     y_up = [jnp.zeros((8, HALF), F32) for _ in range(2)]
     y_dn = [jnp.zeros((8, HALF), F32) for _ in range(2)]
     lane8 = lanes((8, HALF))
@@ -181,9 +202,11 @@
                         y_dn[k] = jnp.where(lane8 == at, roll(out[Y_DN[n]], at, 1), y_dn[k])
                     at = 32 * n + 16 * h + 8 * k
                     if x == 3:
-                        xp[at : at + 8, :] = out[X_UP[n]]
+                        up, dn = out[X_UP[n]], face[at : at + 8, :]
+                        xa[at : at + 8, :] = jnp.where(paired, up, dn)
+                        xb[at : at + 8, :] = jnp.where(paired, dn, up)
                     if x == 0:
-                        xm[at : at + 8, :] = out[X_DN[n]]
+                        face[at : at + 8, :] = out[X_DN[n]]
     for k in range(2):
         yp[8 * k : 8 * k + 8, :] = y_up[k]
         ym[8 * k : 8 * k + 8, :] = y_dn[k]
@@ -191,16 +214,19 @@
         copy.wait()
 
 
-def y_kernel(yp, ym, zbuf, zin, outp, outm):
+def y_kernel(yp, ym, zbuf, zin, outa, outb):
     low = lax.axis_index("gz") == 0
+    paired = even("gy")
     lane = lanes((1, HALF))
     sent = zin[Z_E + 4 : Z_E + 5, :]
     row = jnp.where((lane >= 32) & low, zbuf[Z_E + 4 : Z_E + 5, :], sent)
-    for out, edge, first in ((outp, yp, 20 + 12), (outm, ym, 16)):
-        out[0:16, :] = edge[...]
+    up, dn = yp[...], ym[...]
+    c_up, c_dn = zin[32:36, :], zin[16:20, :]
+    for out, own_up in ((outa, paired), (outb, jnp.logical_not(paired))):
+        out[0:16, :] = jnp.where(own_up, up, dn)
         out[Y_S : Y_S + 16, :] = zin[Z_S : Z_S + 16, :]
         out[Y_E : Y_E + 8, :] = jnp.broadcast_to(row, (8, HALF))
-        out[Y_D : Y_D + 4, :] = zin[first : first + 4, :]
+        out[Y_D : Y_D + 4, :] = jnp.where(own_up, c_up, c_dn)
         out[Y_D + 4 : Y_D + 8, :] = jnp.zeros((4, HALF), F32)
 
 
@@ -210,22 +236,29 @@
     return left, right
 
 
-def x_kernel(inp, inm, zin, ypin, ymin, misc, outp, outm):
+def x_kernel(ina, inb, zin, ya, yb, misc, pops, outa, outb, ypin, ymin):
     low = lax.axis_index("gz") == 0
+    paired = even("gy")
+    ypin[...] = jnp.where(paired, yb[...], ya[...])
+    ymin[...] = jnp.where(paired, ya[...], yb[...])
     left, right = halo_slabs(low, zin, ypin, ymin)
     warm = jnp.where(low, misc[8:12, :], zin[Z_E : Z_E + 4, :])
     lane = lanes((16, HALF))
-    for out, x, n, up, dn in ((outp, 3, 1, 7, 9), (outm, 0, 2, 10, 8)):
+    tails = []
+    for x, n, up, dn in ((3, 1, 7, 9), (0, 2, 10, 8)):
         k_up, k_dn = 4 * Y_UP.index(up) + x, 4 * Y_DN.index(dn) + x + 1
         slab = jnp.where((lane & 15) == 4 * x + 1, left, right)
         slab = jnp.where(lane == k_up, ypin[0:16, :], slab)
-        out[X_T : X_T + 16, :] = jnp.where(lane == k_dn, roll(ymin[0:16, :], 1, 1), slab)
-        for h in range(2):
-            row = 20 * h + 4 * n + x
-            out[X_R + h : X_R + h + 1, :] = zin[row : row + 1, :]
-        out[X_R + 2 : X_R + 3, :] = misc[x : x + 1, :]
-        out[X_R + 3 : X_R + 4, :] = misc[4 + x : 5 + x, :]
-        out[X_R + 4 : X_R + 5, :] = warm[x : x + 1, :]
+        slab = jnp.where(lane == k_dn, roll(ymin[0:16, :], 1, 1), slab)
+        at = 4 * n + x
+        tails.append((slab, zin[at : at + 1, :], zin[20 + at : 21 + at, :],
+                      misc[x : x + 1, :], misc[4 + x : 5 + x, :], warm[x : x + 1, :]))
+    paired = even("gx")
+    for out, (first, second) in ((outa, (0, 1)), (outb, (1, 0))):
+        parts = [jnp.where(paired, u, v) for u, v in zip(tails[first], tails[second])]
+        out[X_T : X_T + 16, :] = parts[0]
+        for k in range(5):
+            out[X_R + k : X_R + k + 1, :] = parts[1 + k]
         out[X_R + 5 : X_R + 8, :] = jnp.zeros((3, HALF), F32)
 
 
@@ -312,11 +345,109 @@
     put_inside(SIDE, low, out, buf, sems, post, zin, ypin, ymin, None, None, nozzle, wall)
 
 
+def spread(folded, at):
+    return jnp.concatenate([roll(folded, at - 32 * g, 1) for g in range(4)], axis=0)
+
+
+def vertical(c):
+    down = jnp.where(rows_of((DEPTH, HALF)) == DEPTH - 1, 0.0, 0.5 * (c + roll(c, -1, 0)))
+    return down, roll(down, 1, 0)
+
+
+def around(*links):
+    total = None
+    for link, value in links:
+        total = link * value if total is None else total + link * value
+    return total
+
+
+def beside_of(value, left_col, right_col):
+    lane = lanes((DEPTH, HALF))
+    return (
+        jnp.where(lane == 0, left_col, roll(value, 1, 1)),
+        jnp.where(lane == HALF - 1, right_col, roll(value, -1, 1)),
+    )
+
+
+def columns(pair, x):
+    at = (4 * x) % HALF
+    return roll(pair[0], -at, 1), roll(pair[1], HALF - 1 - at, 1)
+
+
+def sources(u, load, cool, warm):
+    depth = rows_of((DEPTH, HALF))
+    floor, face = depth == 0, depth == DEPTH - 1
+    base = u + jnp.where(floor, load, 0.0) + jnp.where(face, warm * cool, 0.0)
+    return base, 1.0 + jnp.where(face, warm, 0.0)
+
+
+def sink_kernel(temp, cond, own, misc, zbuf, zin, ypin, ymin, cell, edge):
+    low = lax.axis_index("gz") == 0
+    lane = lanes((DEPTH, HALF))
+    left, right = halo_slabs(low, zin, ypin, ymin)
+    own_edges = own[...]
+    row_left = jnp.where(low, ypin[Y_E : Y_E + 1, :], zin[Z_E + 4 : Z_E + 5, :])
+    row_right = jnp.where(low, zin[Z_E + 4 : Z_E + 5, :], ymin[Y_E : Y_E + 1, :])
+    heat_left = jnp.where(low, roll(row_left, -48, 1), roll(row_left, -32, 1))
+    heat_right = jnp.where(low, roll(zbuf[Z_E + 4 : Z_E + 5, :], -49, 1), roll(row_right, -33, 1))
+    pair_u, pair_c, pair_f = [], [], []
+    for side, (folded, j1, j2, jo, row, h_row, jr) in enumerate((
+        (left, 1, 0, 2, row_left, heat_left, 0),
+        (right, 2, 3, 1, row_right, heat_right, 1),
+    )):
+        u1, u2 = spread(folded, -j1), spread(folded, -j2)
+        c1, c2 = spread(folded, -16 - j1), spread(folded, -16 - j2)
+        uo, co = roll(own_edges, -jo, 1), roll(own_edges, -16 - jo, 1)
+        g_far, g_own = 0.5 * (c1 + c2), 0.5 * (c1 + co)
+        g_up = jnp.where(lane < 12, 0.5 * (c1 + roll(c1, -4, 1)), 0.0)
+        g_dn = jnp.where(lane >= 4, roll(g_up, 4, 1), 0.0)
+        v_dn, v_up = vertical(c1)
+        base, rest = sources(u1, roll(row, -jr, 1), roll(row, -16 - jr, 1), h_row)
+        den = rest + (g_far + g_own) + (g_up + g_dn) + (v_dn + v_up)
+        num = base + around((g_far, u2), (g_own, uo), (g_up, roll(u1, -4, 1)), (g_dn, roll(u1, 4, 1)),
+                            (v_dn, roll(u1, -1, 0)), (v_up, roll(u1, 1, 0)))
+        edge[side, 0], edge[side, 1], edge[side, 2], edge[side, 3] = u1, c1, num, den
+        pair_u.append(u1)
+        pair_c.append(c1)
+        pair_f.append(num / den)
+    warm = jnp.where(low, misc[8:12, :], zin[Z_E : Z_E + 4, :])
+    g_x = {x: 0.5 * (cond[x] + cond[x + 1]) for x in range(SX - 1)}
+    first, inverse = {}, {}
+    for x in range(SX):
+        u, c = temp[x], cond[x]
+        c_l, c_r = beside_of(c, *columns(pair_c, x))
+        u_l, u_r = beside_of(u, *columns(pair_u, x))
+        g_l, g_r = 0.5 * (c + c_l), 0.5 * (c + c_r)
+        v_dn, v_up = vertical(c)
+        base, den = sources(u, misc[x : x + 1, :], misc[4 + x : 5 + x, :], warm[x : x + 1, :])
+        den = den + (g_l + g_r) + (v_dn + v_up)
+        num = base + around((g_l, u_l), (g_r, u_r), (v_dn, roll(u, -1, 0)), (v_up, roll(u, 1, 0)))
+        if x > 0:
+            den, num = den + g_x[x - 1], num + g_x[x - 1] * temp[x - 1]
+        if x < SX - 1:
+            den, num = den + g_x[x], num + g_x[x] * temp[x + 1]
+        for k, value in enumerate((num, den, base, g_l, g_r, v_dn)):
+            cell[k, x] = value
+        if 0 < x < SX - 1:
+            inverse[x] = 1.0 / den
+            first[x] = num * inverse[x]
+    for x, other in ((1, 2), (2, 1)):
+        f = first[x]
+        f_l, f_r = beside_of(f, *columns(pair_f, x))
+        v_dn = cell[5, x]
+        num = cell[2, x] + g_x[1] * first[other] + around(
+            (cell[3, x], f_l), (cell[4, x], f_r), (v_dn, roll(f, -1, 0)), (roll(v_dn, 1, 0), roll(f, 1, 0)))
+        cell[0, x], cell[1, x], cell[2, x] = f, inverse[x], num
+
+
 def final_kernel(
-    whole, post, zin, ypin, ymin, xpin, xmin, nozzle, wall, temp, cond, own, misc, zbuf,
-    pops_out, solid_out, buf, solid, sems,
+    whole, post, zin, ypin, ymin, xb, xa, nozzle, wall, temp, cond, cell, edges,
+    pops_out, solid_out, xpin, xmin, buf, solid, sems,
 ):
     low = lax.axis_index("gz") == 0
+    paired = even("gx")
+    xpin[...] = jnp.where(paired, xb[...], xa[...])
+    xmin[...] = jnp.where(paired, xa[...], xb[...])
     copies = []
     for i, v in enumerate(X_UP + X_DN):
         x = 0 if i < 5 else SX - 1
@@ -326,113 +457,60 @@
         copies[-1].start()
 
     lane = lanes((DEPTH, HALF))
-    depth = rows_of((DEPTH, HALF))
-    floor, face = depth == 0, depth == DEPTH - 1
-
-    def spread(folded, at):
-        return jnp.concatenate([roll(folded, at - 32 * g, 1) for g in range(4)], axis=0)
-
-    def vertical(c):
-        down = jnp.where(face, 0.0, 0.5 * (c + roll(c, -1, 0)))
-        return down, roll(down, 1, 0)
-
-    def around(links):
-        total = None
-        for link, value in links:
-            total = link * value if total is None else total + link * value
-        return total
-
-    U = {x: temp[x] for x in range(SX)}
-    C = {x: cond[x] for x in range(SX)}
-    for near, far, edge in ((-1, -2, xpin), (4, 5, xmin)):
-        U[near], U[far] = edge[X_U : X_U + 64, :], edge[X_U + 64 : X_U + 128, :]
-        C[near], C[far] = edge[X_U + 128 : X_U + 192, :], edge[X_U + 192 : X_U + 256, :]
-    warm = jnp.where(low, misc[8:12, :], zin[Z_E : Z_E + 4, :])
-    loads = {x: misc[x : x + 1, :] for x in range(SX)}
-    cools = {x: misc[4 + x : 5 + x, :] for x in range(SX)}
-    warms = {x: warm[x : x + 1, :] for x in range(SX)}
-    for x, edge in ((-1, xpin), (4, xmin)):
-        loads[x], cools[x], warms[x] = (edge[X_R + 2 + k : X_R + 3 + k, :] for k in range(3))
-
-    left, right = halo_slabs(low, zin, ypin, ymin)
-    own_edges = own[...]
-    near_first = {}
-    side = {}
-    row_left = jnp.where(low, ypin[Y_E : Y_E + 1, :], zin[Z_E + 4 : Z_E + 5, :])
-    row_right = jnp.where(low, zin[Z_E + 4 : Z_E + 5, :], ymin[Y_E : Y_E + 1, :])
-    heat_left = jnp.where(low, roll(row_left, -48, 1), roll(row_left, -32, 1))
-    heat_right = jnp.where(low, roll(zbuf[Z_E + 4 : Z_E + 5, :], -49, 1), roll(row_right, -33, 1))
     before, after = xpin[X_T : X_T + 16, :], xmin[X_T : X_T + 16, :]
-    for name, folded, j1, j2, jo, row, h_row, jr in (
-        ("left", left, 1, 0, 2, row_left, heat_left, 0),
-        ("right", right, 2, 3, 1, row_right, heat_right, 1),
-    ):
-        u1, u2 = spread(folded, -j1), spread(folded, -j2)
-        c1, c2 = spread(folded, -16 - j1), spread(folded, -16 - j2)
-        u1 = jnp.where(lane == 124, spread(before, 124 - 12 - j1), jnp.where(lane == 16, spread(after, 16 - j1), u1))
-        c1 = jnp.where(lane == 124, spread(before, 124 - 28 - j1), jnp.where(lane == 16, spread(after, -j1), c1))
-        side[name] = (u1, c1)
-        uo, co = roll(own_edges, -jo, 1), roll(own_edges, -16 - jo, 1)
-        g_far, g_own = 0.5 * (c1 + c2), 0.5 * (c1 + co)
+    pair_u, pair_c, pair_f = [], [], []
+    for side, j in ((0, 1), (1, 2)):
+        u1, c1 = edges[side, 0], edges[side, 1]
+        u1 = jnp.where(lane == 124, spread(before, 112 - j), jnp.where(lane == 16, spread(after, 16 - j), u1))
+        c1 = jnp.where(lane == 124, spread(before, 96 - j), jnp.where(lane == 16, spread(after, -j), c1))
         g_up = 0.5 * (c1 + roll(c1, -4, 1))
-        g_dn = roll(g_up, 4, 1)
-        v_dn, v_up = vertical(c1)
-        e_load, e_cool = roll(row, -jr, 1), roll(row, -16 - jr, 1)
-        num = u1 + jnp.where(floor, e_load, 0.0) + jnp.where(face, h_row * e_cool, 0.0)
-        den = 1.0 + jnp.where(face, h_row, 0.0) + (g_far + g_own) + (g_up + g_dn) + (v_dn + v_up)
-        num = num + around(((g_far, u2), (g_own, uo), (g_up, roll(u1, -4, 1)), (g_dn, roll(u1, 4, 1)),
-                            (v_dn, roll(u1, -1, 0)), (v_up, roll(u1, 1, 0))))
-        near_first[name] = num / den
-
-    def beside_of(value, left_col, right_col):
-        return (
-            jnp.where(lane == 0, left_col, roll(value, 1, 1)),
-            jnp.where(lane == HALF - 1, right_col, roll(value, -1, 1)),
-        )
-
-    def columns(pair, x):
-        at = (4 * x) % HALF
-        return roll(pair[0], -at, 1), roll(pair[1], HALF - 1 - at, 1)
-
-    pair_u = (side["left"][0], side["right"][0])
-    pair_c = (side["left"][1], side["right"][1])
-    pair_f = (near_first["left"], near_first["right"])
-    g_x = {x: 0.5 * (C[x] + C[x + 1]) for x in range(-2, 5)}
-    first, kept = {}, {}
-    for x in range(-1, 5):
-        c_l, c_r = beside_of(C[x], *columns(pair_c, x))
-        u_l, u_r = beside_of(U[x], *columns(pair_u, x))
-        g_l, g_r = 0.5 * (C[x] + c_l), 0.5 * (C[x] + c_r)
-        v_dn, v_up = vertical(C[x])
-        base = U[x] + jnp.where(floor, loads[x], 0.0) + jnp.where(face, warms[x] * cools[x], 0.0)
-        den = 1.0 + jnp.where(face, warms[x], 0.0) + (g_x[x - 1] + g_x[x]) + (g_l + g_r) + (v_dn + v_up)
-        inv = 1.0 / den
-        num = base + around(((g_x[x - 1], U[x - 1]), (g_x[x], U[x + 1]), (g_l, u_l), (g_r, u_r),
-                             (v_dn, roll(U[x], -1, 0)), (v_up, roll(U[x], 1, 0))))
-        first[x] = num * inv
-        kept[x] = (base, inv, g_l, g_r, v_dn, v_up)
-    for x in range(SX):
-        base, inv, g_l, g_r, v_dn, v_up = kept[x]
-        f_l, f_r = beside_of(first[x], *columns(pair_f, x))
-        num = base + around(((g_x[x - 1], first[x - 1]), (g_x[x], first[x + 1]), (g_l, f_l), (g_r, f_r),
-                             (v_dn, roll(first[x], -1, 0)), (v_up, roll(first[x], 1, 0))))
-        solid[x] = num * inv
-        copies.append(pltpu.make_async_copy(solid.at[x], solid_out.at[x], sems.at[10 + x]))
-        copies[-1].start()
+        g_dn = jnp.where(lane == 0, roll(g_up, 4, 1), 0.0)
+        g_up = jnp.where(lane == 12, g_up, 0.0)
+        num = edges[side, 2] + around((g_up, roll(u1, -4, 1)), (g_dn, roll(u1, 4, 1)))
+        pair_u.append(u1)
+        pair_c.append(c1)
+        pair_f.append(num / (edges[side, 3] + g_up + g_dn))
+    first, inverse, g_x = {1: cell[0, 1], 2: cell[0, 2]}, {1: cell[1, 1], 2: cell[1, 2]}, {}
+    for side, x, n, inner in ((xpin, -1, 0, 1), (xmin, 4, 3, 2)):
+        u, u_far = side[X_U : X_U + 64, :], side[X_U + 64 : X_U + 128, :]
+        c, c_far = side[X_U + 128 : X_U + 192, :], side[X_U + 192 : X_U + 256, :]
+        link, g_far = 0.5 * (c + cond[n]), 0.5 * (c + c_far)
+        c_l, c_r = beside_of(c, *columns(pair_c, x))
+        u_l, u_r = beside_of(u, *columns(pair_u, x))
+        g_l, g_r = 0.5 * (c + c_l), 0.5 * (c + c_r)
+        v_dn, v_up = vertical(c)
+        base, den = sources(u, *(side[X_R + 2 + k : X_R + 3 + k, :] for k in range(3)))
+        den = den + (link + g_far) + (g_l + g_r) + (v_dn + v_up)
+        num = base + around((g_far, u_far), (link, temp[n]), (g_l, u_l), (g_r, u_r),
+                            (v_dn, roll(u, -1, 0)), (v_up, roll(u, 1, 0)))
+        outer = num / den
+        inverse[n] = 1.0 / (cell[1, n] + link)
+        first[n] = (cell[0, n] + link * u) * inverse[n]
+        f = first[n]
+        f_l, f_r = beside_of(f, *columns(pair_f, n))
+        v_dn = cell[5, n]
+        g_x[inner] = 0.5 * (cond[n] + cond[inner])
+        num = cell[2, n] + link * outer + g_x[inner] * first[inner] + around(
+            (cell[3, n], f_l), (cell[4, n], f_r), (v_dn, roll(f, -1, 0)), (roll(v_dn, 1, 0), roll(f, 1, 0)))
+        solid[n] = num * inverse[n]
+        solid[inner] = (cell[2, inner] + g_x[inner] * f) * inverse[inner]
+        for k in (n, inner):
+            copies.append(pltpu.make_async_copy(solid.at[k], solid_out.at[k], sems.at[10 + k]))
+            copies[-1].start()
     for copy in copies:
         copy.wait()
 
 
 def shape(*dims):
-    return jax.ShapeDtypeStruct(dims, F32)
+    return pltpu.HBM(dims, F32)
 
 
 def near(*dims):
     return pltpu.VMEM(dims, F32)
 
 
-def hold(*arrays):
-    return [pltpu.with_memory_space_constraint(a, pltpu.VMEM) for a in arrays]
+def hold(array, kind):
+    return pltpu.with_memory_space_constraint(array, pltpu.VMEM if kind == "near" else pltpu.HBM)
 
 
 VM = pl.BlockSpec(memory_space=pltpu.VMEM)
@@ -444,17 +522,23 @@
     return [(i, (i + step) % n) for i in range(n)]
 
 
+def pairs(axis, odd):
+    n = lax.axis_size(axis)
+    return [(i, (i + 1) % n if i % 2 == odd else (i - 1) % n) for i in range(n)]
+
+
 def call(kernel, name, inputs, outputs, scratch=(), aliases=None):
     spaces = [ANY if kind == "far" else VM for kind, _ in inputs]
-    arrays = [hold(a)[0] if kind == "near" else a for kind, a in inputs]
+    arrays = [hold(a, kind) for kind, a in inputs]
     return pl.pallas_call(
         kernel,
         name=name,
         in_specs=spaces,
-        out_specs=[ANY if isinstance(o, jax.ShapeDtypeStruct) else VM for o in outputs],
+        out_specs=[ANY if o.memory_space == pltpu.HBM else VM for o in outputs],
         out_shape=list(outputs),
         scratch_shapes=list(scratch),
         input_output_aliases=aliases or {},
+        compiler_params=pltpu.CompilerParams(vmem_limit_bytes=16 * 1024 * 1024),
     )(*arrays)
 
 
@@ -475,34 +559,40 @@
         [pltpu.VMEM((2, 19, 8, HALF), F32), dma((8,))],
     )
     zin = lax.ppermute(zbuf, "gz", ring("gz", 1))
-    post, yp, ym, xp, xm, nozzle, wall = call(
+    post, yp, ym, xa, xb, nozzle, wall = call(
         collide_kernel, "collide",
         far(populations, nozzle_mask, wall_type) + kept(temp, cond),
         [near(19, SX, SZ_, 2 * HALF), near(16, HALF), near(16, HALF), near(X_ROWS, HALF), near(X_ROWS, HALF),
          pltpu.VMEM((SX, 2 * HALF), jnp.int32), pltpu.VMEM((SX, 2 * HALF), jnp.int32)],
-        [pltpu.VMEM((19, SX, SZ_, 2 * HALF), F32), dma((SX + 2,))],
-    )
-    ypo, ymo = call(y_kernel, "pack_y", kept(yp, ym, zbuf, zin), [near(Y_ROWS, HALF)] * 2)
-    ypin = lax.ppermute(ypo, "gy", ring("gy", 1))
-    ymin = lax.ppermute(ymo, "gy", ring("gy", -1))
+        [pltpu.VMEM((19, SX, SZ_, 2 * HALF), F32), pltpu.VMEM((X_U, HALF), F32), dma((SX + 2,))],
+    )
+    yao, ybo = call(y_kernel, "pack_y", kept(yp, ym, zbuf, zin), [near(Y_ROWS, HALF)] * 2)
+    ya = lax.ppermute(yao, "gy", pairs("gy", 0))
+    yb = lax.ppermute(ybo, "gy", pairs("gy", 1))
     (pops,) = call(
         inner_kernel, "inner", kept(post, zin, nozzle, wall), [shape(19, SX, SZ_, 2 * HALF)],
         [pltpu.VMEM((len(INNER), SX, SZ_, 2 * HALF), F32), dma((len(INNER),))],
     )
-    xpo, xmo = call(
-        x_kernel, "pack_x", kept(xp, xm, zin, ypin, ymin, misc), [near(X_ROWS, HALF)] * 2, aliases={0: 0, 1: 1}
-    )
-    xpin = lax.ppermute(xpo, "gx", ring("gx", 1))
-    xmin = lax.ppermute(xmo, "gx", ring("gx", -1))
+    xao, xbo, ypin, ymin = call(
+        x_kernel, "pack_x", kept(xa, xb, zin, ya, yb, misc) + far(pops),
+        [near(X_ROWS, HALF)] * 2 + [near(Y_ROWS, HALF)] * 2, aliases={0: 0, 1: 1},
+    )
+    xa = lax.ppermute(xao, "gx", pairs("gx", 0))
+    xb = lax.ppermute(xbo, "gx", pairs("gx", 1))
+    cell, edge = call(
+        sink_kernel, "sink", kept(temp, cond, own, misc, zbuf, zin, ypin, ymin),
+        [near(6, SX, DEPTH, HALF), near(2, 4, DEPTH, HALF)],
+    )
     (pops,) = call(
         side_kernel, "side", far(pops) + kept(post, zin, ypin, ymin, nozzle, wall), [shape(19, SX, SZ_, 2 * HALF)],
         [pltpu.VMEM((len(SIDE), SX, SZ_, 2 * HALF), F32), dma((len(SIDE),))], {0: 0},
     )
     return tuple(call(
         final_kernel, "finish",
-        far(pops) + kept(post, zin, ypin, ymin, xpin, xmin, nozzle, wall, temp, cond, own, misc, zbuf),
+        far(pops) + kept(post, zin, ypin, ymin, xb, xa, nozzle, wall, temp, cond, cell, edge),
         [shape(19, SX, SZ_, 2 * HALF), shape(SX, DEPTH, HALF)],
-        [pltpu.VMEM((10, SZ_, 2 * HALF), F32), pltpu.VMEM((SX, DEPTH, HALF), F32), dma((14,))], {0: 0},
+        [pltpu.VMEM((X_ROWS, HALF), F32), pltpu.VMEM((X_ROWS, HALF), F32),
+         pltpu.VMEM((10, SZ_, 2 * HALF), F32), pltpu.VMEM((SX, DEPTH, HALF), F32), dma((14,))], {0: 0},
     ))
 
 

time: 41.1 us -> 39.9 us (0.971)
  the two profiles are of different devices: /device:TPU:62 before, /device:TPU:64 now
where the time goes in v3:
time: 39.9 us; the launch traced here: 39.6 us
  starting transfers between devices  25 us (63%)
  Pallas kernels  7.36 us (18%)
  waiting for transfers between devices  6.52 us (16%)
  between operations  0.72 us (2%)
    ppermute x1, starting transfers between devices, body(): zin = lax.ppermute(zbuf, 'gz', ring('gz', 1))  9.99 us
    pallas_call x8, Pallas kernels, call(): pl.pallas_call(kernel, name=name, in_specs=spaces, out_specs=[ANY if o.me...  7.36 us
    ppermute x1, starting transfers between devices, body(): xb = lax.ppermute(xbo, 'gx', pairs('gx', 1))  6.35 us
    ppermute x1, starting transfers between devices, body(): yb = lax.ppermute(ybo, 'gy', pairs('gy', 1))  4.85 us
    ppermute x1, waiting for transfers between devices, body(): xa = lax.ppermute(xao, 'gx', pairs('gx', 0))  3.37 us
    ppermute x1, waiting for transfers between devices, body(): xb = lax.ppermute(xbo, 'gx', pairs('gx', 1))  2.47 us
    ppermute x1, starting transfers between devices, body(): ya = lax.ppermute(yao, 'gy', pairs('gy', 0))  1.92 us
    ppermute x1, starting transfers between devices, body(): xa = lax.ppermute(xao, 'gx', pairs('gx', 0))  1.92 us
  transfers between devices with their start and end apart: 5, of which 4 were waited for; matrix products, arithmetic and copies ran while one was open for 0% of the time, Pallas kernels for 11%

profile of v3, /device:TPU:64, one launch (start us, length us, event | category | flops | bytes accessed | tf_op | source)
XLA Modules:
  0.0 39.6 jit_solution(2805312847978191993)
XLA Ops:
  0.6 1.4 %face.1 = (f32[64,128]{1,0:T(8,128)S(1)}, f32[64,128]{1,0:T(8,128)S(1)}, f32[16,128]{1,0:T(8,128)S(1)}, f32[4,64,128]{2,1,0:T(8,128)S(1)}, f32[4,64,128]{2,1,0:T(8,128)S(1)}) custom-call(f32[19,4,16,256]{3,2,1,0:T(8,128)} %pops.3, f32[4,64,128]{2,1,0:T(8,128)} %temp.1, f32[4,64,128]{2,1,0:T(8,128)} %cond.1, f32[4,128]{1,0:T(4,128)} %load.1, f32[4,128]{1,0:T(4,128)} %cool.1), custom_call_target="tpu_custom_call" | custom-call | tf_op jit(solution)/shard_map/face/pallas_call | solution.py:533
  2.1 10.0 %collective-permute-start = (f32[64,128]{1,0:T(8,128)S(1)}, f32[64,128]{1,0:T(8,128)S(1)}, u32[]{:S(2)}, u32[]{:S(2)}) collective-permute-start(f32[64,128]{1,0:T(8,128)S(1)} %get-tuple-element.25.zbuf), channel_id=1, source_target_pairs={{0,1},{1,0},{2,3},{3,2},{4,5},{5,4},{6,7},{7,6},{8,9},{9,8},{10,11... | collective-permute-start | bytes 98312 | tf_op jit(solution)/shard_map/ppermute | solution.py:561
  12.1 1.8 %collide.1 = (f32[19,4,16,256]{3,2,1,0:T(8,128)S(1)}, f32[16,128]{1,0:T(8,128)S(1)}, f32[16,128]{1,0:T(8,128)S(1)}, f32[440,128]{1,0:T(8,128)S(1)}, f32[440,128]...) custom-call(f32[19,4,16,256]{3,2,1,0:T(8,128)} %pops.3, s32[4,256]{1,0:T(4,128)} %nozzle.1, s32[4,256]{1,0:T(4,128)} %wall.1, ...), custom_call_target="tpu_custom_call" | custom-call | tf_op jit(solution)/shard_map/collide/pallas_call | solution.py:533
  13.9 0.1 collective-permute-done.zin
  14.0 1.9 %collective-permute-start.1 = (f32[48,128]{1,0:T(8,128)S(1)}, f32[48,128]{1,0:T(8,128)S(1)}, u32[]{:S(2)}, u32[]{:S(2)}) collective-permute-start(f32[48,128]{1,0:T(8,128)S(1)} %get-tuple-element.32), channel_id=1, source_target_pairs={{0,2},{2,0},{4,6},{6,4},{8,10},{10,8},{12,14},{14,12},{1,3},{3,1},... | collective-permute-start | bytes 73736 | tf_op jit(solution)/shard_map/ppermute | solution.py:570
  15.9 4.8 %collective-permute-start.2 = (f32[48,128]{1,0:T(8,128)S(1)}, f32[48,128]{1,0:T(8,128)S(1)}, u32[]{:S(2)}, u32[]{:S(2)}) collective-permute-start(f32[48,128]{1,0:T(8,128)S(1)} %get-tuple-element.33), channel_id=1, source_target_pairs={{0,14},{2,4},{4,2},{6,8},{8,6},{10,12},{12,10},{14,0},{1,15},{3,5}... | collective-permute-start | bytes 73736 | tf_op jit(solution)/shard_map/ppermute | solution.py:571
  20.8 0.8 %inner.1.pops.whole = f32[19,4,16,256]{3,2,1,0:T(8,128)} custom-call(f32[19,4,16,256]{3,2,1,0:T(8,128)S(1)} %get-tuple-element.24.post, f32[64,128]{1,0:T(8,128)S(1)} %collective-permute-done.zin, s32[4,256]{1,0:T(4,128)S(1)} %get-tuple-element.26.nozzle, s32[4,256]{1,0:T(4,128)S(1)} %get-tuple-element.27.wall), custom_call_target="tpu_custom_call" | custom-call | tf_op jit(solution)/shard_map/inner/pallas_call | solution.py:533
  21.6 0.0 collective-permute-done.1.ya
  21.6 0.6 %collective-permute-done.2.yb = f32[48,128]{1,0:T(8,128)S(1)} collective-permute-done((f32[48,128]{1,0:T(8,128)S(1)}, f32[48,128]{1,0:T(8,128)S(1)}, u32[]{:S(2)}, u32[]{:S(2)}) %collective-permute-start.2) | collective-permute-done | bytes 24608 | tf_op jit(solution)/shard_map/ppermute | solution.py:571
  22.3 0.1 pack_x.1
  22.3 6.4 %collective-permute-start.3 = (f32[440,128]{1,0:T(8,128)S(1)}, f32[440,128]{1,0:T(8,128)S(1)}, u32[]{:S(2)}, u32[]{:S(2)}) collective-permute-start(f32[440,128]{1,0:T(8,128)S(1)} %get-tuple-element.37), channel_id=1, source_target_pairs={{0,496},{16,32},{32,16},{48,64},{64,48},{80,96},{96,80},{112,128},... | collective-permute-start | bytes 675848 | tf_op jit(solution)/shard_map/ppermute | solution.py:581
  28.7 1.9 %collective-permute-start.4 = (f32[440,128]{1,0:T(8,128)S(1)}, f32[440,128]{1,0:T(8,128)S(1)}, u32[]{:S(2)}, u32[]{:S(2)}) collective-permute-start(f32[440,128]{1,0:T(8,128)S(1)} %get-tuple-element.38), channel_id=1, source_target_pairs={{0,16},{16,0},{32,48},{48,32},{64,80},{80,64},{96,112},{112,96},{1... | collective-permute-start | bytes 675848 | tf_op jit(solution)/shard_map/ppermute | solution.py:580
  30.6 1.0 %side.1.whole = f32[19,4,16,256]{3,2,1,0:T(8,128)} custom-call(f32[19,4,16,256]{3,2,1,0:T(8,128)} %inner.1.pops.whole, f32[19,4,16,256]{3,2,1,0:T(8,128)S(1)} %get-tuple-element.24.post, f32[64,128]{1,0:T(8,128)S(1)} %collective-permute-done.zin, f32[48,128]{1,0:T(8,128)S(1)} %get-tuple-element.35.ypin, ...), custom_call_target="tpu_custom_call", output_to_operand_aliasing={{}: (0, {})} | custom-call | tf_op jit(solution)/shard_map/side/pallas_call | solution.py:533
  31.7 0.7 %sink.1 = (f32[6,4,64,128]{3,2,1,0:T(8,128)S(1)}, f32[2,4,64,128]{3,2,1,0:T(8,128)S(1)}) custom-call(f32[4,64,128]{2,1,0:T(8,128)S(1)} %get-tuple-element.22.tempv.temp, f32[4,64,128]{2,1,0:T(8,128)S(1)} %get-tuple-element.23.condv.cond, f32[64,128]{1,0:T(8,128)S(1)} %get-tuple-element.39.own, f32[16,128]{1,0:T(8,128)S(1)} %get-tuple-element.34.misc, ...), custom_call_target="tpu_custom_call" | custom-call | tf_op jit(solution)/shard_map/sink/pallas_call | solution.py:533
  32.4 2.5 %collective-permute-done.3.xb = f32[440,128]{1,0:T(8,128)S(1)} collective-permute-done((f32[440,128]{1,0:T(8,128)S(1)}, f32[440,128]{1,0:T(8,128)S(1)}, u32[]{:S(2)}, u32[]{:S(2)}) %collective-permute-start.3) | collective-permute-done | bytes 225312 | tf_op jit(solution)/shard_map/ppermute | solution.py:581
  34.9 3.4 %collective-permute-done.4.xa = f32[440,128]{1,0:T(8,128)S(1)} collective-permute-done((f32[440,128]{1,0:T(8,128)S(1)}, f32[440,128]{1,0:T(8,128)S(1)}, u32[]{:S(2)}, u32[]{:S(2)}) %collective-permute-start.4) | collective-permute-done | bytes 225312 | tf_op jit(solution)/shard_map/ppermute | solution.py:580
  38.2 1.4 %finish.1 = (f32[19,4,16,256]{3,2,1,0:T(8,128)}, f32[4,64,128]{2,1,0:T(8,128)}) custom-call(f32[19,4,16,256]{3,2,1,0:T(8,128)} %side.1.whole, f32[19,4,16,256]{3,2,1,0:T(8,128)S(1)} %get-tuple-element.24.post, f32[64,128]{1,0:T(8,128)S(1)} %collective-permute-done.zin, f32[48,128]{1,0:T(8,128)S(1)} %get-tuple-element.35.ypin, ...), custom_call_target="tpu_custom_call", output_to_operand_aliasing={{0}: (0, {})} | custom-call | tf_op jit(solution)/shard_map/finish/pallas_call | solution.py:533
  (1 shorter events, 0.0 us)
Async XLA Ops:
  2.1 11.9 %collective-permute-start = (f32[64,128]{1,0:T(8,128)S(1)}, f32[64,128]{1,0:T(8,128)S(1)}, u32[]{:S(2)}, u32[]{:S(2)}) collective-permute-start(f32[64,128]{1,0:T(8,128)S(1)} %get-tuple-element.25.zbuf), channel_id=1, source_target_pairs={{0,1},{1,0},{2,3},{3,2},{4,5},{5,4},{6,7},{7,6},{8,9},{9,8},{10,11... | collective-permute-start | bytes 98312 | tf_op jit(solution)/shard_map/ppermute | solution.py:561
  14.0 7.6 %collective-permute-start.1 = (f32[48,128]{1,0:T(8,128)S(1)}, f32[48,128]{1,0:T(8,128)S(1)}, u32[]{:S(2)}, u32[]{:S(2)}) collective-permute-start(f32[48,128]{1,0:T(8,128)S(1)} %get-tuple-element.32), channel_id=1, source_target_pairs={{0,2},{2,0},{4,6},{6,4},{8,10},{10,8},{12,14},{14,12},{1,3},{3,1},... | collective-permute-start | bytes 73736 | tf_op jit(solution)/shard_map/ppermute | solution.py:570
  15.9 6.4 %collective-permute-start.2 = (f32[48,128]{1,0:T(8,128)S(1)}, f32[48,128]{1,0:T(8,128)S(1)}, u32[]{:S(2)}, u32[]{:S(2)}) collective-permute-start(f32[48,128]{1,0:T(8,128)S(1)} %get-tuple-element.33), channel_id=1, source_target_pairs={{0,14},{2,4},{4,2},{6,8},{8,6},{10,12},{12,10},{14,0},{1,15},{3,5}... | collective-permute-start | bytes 73736 | tf_op jit(solution)/shard_map/ppermute | solution.py:571
  22.3 12.5 %collective-permute-start.3 = (f32[440,128]{1,0:T(8,128)S(1)}, f32[440,128]{1,0:T(8,128)S(1)}, u32[]{:S(2)}, u32[]{:S(2)}) collective-permute-start(f32[440,128]{1,0:T(8,128)S(1)} %get-tuple-element.37), channel_id=1, source_target_pairs={{0,496},{16,32},{32,16},{48,64},{64,48},{80,96},{96,80},{112,128},... | collective-permute-start | bytes 675848 | tf_op jit(solution)/shard_map/ppermute | solution.py:581
  28.7 9.5 %collective-permute-start.4 = (f32[440,128]{1,0:T(8,128)S(1)}, f32[440,128]{1,0:T(8,128)S(1)}, u32[]{:S(2)}, u32[]{:S(2)}) collective-permute-start(f32[440,128]{1,0:T(8,128)S(1)} %get-tuple-element.38), channel_id=1, source_target_pairs={{0,16},{16,0},{32,48},{48,32},{64,80},{80,64},{96,112},{112,96},{1... | collective-permute-start | bytes 675848 | tf_op jit(solution)/shard_map/ppermute | solution.py:580

commit v4 on v3

--- a/solution.py
+++ b/solution.py
@@ -97,6 +97,15 @@
     return (lax.axis_index(axis) & 1) == 0
 
 
+def odd_first(y):
+    return (y < 2) | (y % 2 == 0)
+
+
+def checker():
+    odd = odd_first(lax.axis_index("gy"))
+    return (lax.axis_index("gx") & 1) == jnp.where(odd, 1, 0)
+
+
 def face_kernel(pops, temp, cond, load, cool, zbuf, own, misc, tempv, condv, buf, sems):
     low = lax.axis_index("gz") == 0
     face = jnp.where(low, SZ_ - 1, 0)
@@ -175,7 +184,7 @@
     ]
     for copy in copies + plates:
         copy.start()
-    paired = even("gx")
+    paired = checker()
     for k, field in enumerate((tempv, condv)):
         for j in range(2):
             at = X_U + 128 * k + 64 * j
@@ -253,7 +262,7 @@
         at = 4 * n + x
         tails.append((slab, zin[at : at + 1, :], zin[20 + at : 21 + at, :],
                       misc[x : x + 1, :], misc[4 + x : 5 + x, :], warm[x : x + 1, :]))
-    paired = even("gx")
+    paired = checker()
     for out, (first, second) in ((outa, (0, 1)), (outb, (1, 0))):
         parts = [jnp.where(paired, u, v) for u, v in zip(tails[first], tails[second])]
         out[X_T : X_T + 16, :] = parts[0]
@@ -441,11 +450,11 @@
 
 
 def final_kernel(
-    whole, post, zin, ypin, ymin, xb, xa, nozzle, wall, temp, cond, cell, edges,
+    whole, post, zin, ypin, ymin, xa, xb, nozzle, wall, temp, cond, cell, edges,
     pops_out, solid_out, xpin, xmin, buf, solid, sems,
 ):
     low = lax.axis_index("gz") == 0
-    paired = even("gx")
+    paired = checker()
     xpin[...] = jnp.where(paired, xb[...], xa[...])
     xmin[...] = jnp.where(paired, xa[...], xb[...])
     copies = []
@@ -527,6 +536,14 @@
     return [(i, (i + 1) % n if i % 2 == odd else (i - 1) % n) for i in range(n)]
 
 
+def checker_pairs(turn):
+    ny, nz = lax.axis_size("gy"), lax.axis_size("gz")
+    return [
+        ((i * ny + y) * nz + z, (j * ny + y) * nz + z)
+        for y in range(ny) for i, j in pairs("gx", (int(odd_first(y)) + turn) % 2) for z in range(nz)
+    ]
+
+
 def call(kernel, name, inputs, outputs, scratch=(), aliases=None):
     spaces = [ANY if kind == "far" else VM for kind, _ in inputs]
     arrays = [hold(a, kind) for kind, a in inputs]
@@ -577,8 +594,8 @@
         x_kernel, "pack_x", kept(xa, xb, zin, ya, yb, misc) + far(pops),
         [near(X_ROWS, HALF)] * 2 + [near(Y_ROWS, HALF)] * 2, aliases={0: 0, 1: 1},
     )
-    xa = lax.ppermute(xao, "gx", pairs("gx", 0))
-    xb = lax.ppermute(xbo, "gx", pairs("gx", 1))
+    xa = lax.ppermute(xao, ("gx", "gy", "gz"), checker_pairs(0))
+    xb = lax.ppermute(xbo, ("gx", "gy", "gz"), checker_pairs(1))
     cell, edge = call(
         sink_kernel, "sink", kept(temp, cond, own, misc, zbuf, zin, ypin, ymin),
         [near(6, SX, DEPTH, HALF), near(2, 4, DEPTH, HALF)],
@@ -589,7 +606,7 @@
     )
     return tuple(call(
         final_kernel, "finish",
-        far(pops) + kept(post, zin, ypin, ymin, xb, xa, nozzle, wall, temp, cond, cell, edge),
+        far(pops) + kept(post, zin, ypin, ymin, xa, xb, nozzle, wall, temp, cond, cell, edge),
         [shape(19, SX, SZ_, 2 * HALF), shape(SX, DEPTH, HALF)],
         [pltpu.VMEM((X_ROWS, HALF), F32), pltpu.VMEM((X_ROWS, HALF), F32),
          pltpu.VMEM((10, SZ_, 2 * HALF), F32), pltpu.VMEM((SX, DEPTH, HALF), F32), dma((14,))], {0: 0},

time: 39.9 us -> 39.5 us (0.990)
  the two profiles are of different devices: /device:TPU:64 before, /device:TPU:8 now
where the time goes in v4:
time: 39.5 us; the launch traced here: 39.3 us
  starting transfers between devices  28 us (71%)
  Pallas kernels  7.35 us (19%)
  waiting for transfers between devices  3.18 us (8%)
  between operations  0.73 us (2%)
    ppermute x1, starting transfers between devices, body(): zin = lax.ppermute(zbuf, 'gz', ring('gz', 1))  10.9 us
    pallas_call x8, Pallas kernels, call(): pl.pallas_call(kernel, name=name, in_specs=spaces, out_specs=[ANY if o.me...  7.35 us
    ppermute x1, starting transfers between devices, body(): xb = lax.ppermute(xbo, ('gx', 'gy', 'gz'), checker_pairs(1))  6.45 us
    ppermute x1, starting transfers between devices, body(): yb = lax.ppermute(ybo, 'gy', pairs('gy', 1))  5.27 us
    ppermute x1, starting transfers between devices, body(): xa = lax.ppermute(xao, ('gx', 'gy', 'gz'), checker_pairs(0))  3.47 us
    ppermute x1, waiting for transfers between devices, body(): xb = lax.ppermute(xbo, ('gx', 'gy', 'gz'), checker_pairs(1))  2.28 us
    ppermute x1, starting transfers between devices, body(): ya = lax.ppermute(yao, 'gy', pairs('gy', 0))  1.92 us
    ppermute x1, waiting for transfers between devices, body(): yb = lax.ppermute(ybo, 'gy', pairs('gy', 1))  0.82 us
  transfers between devices with their start and end apart: 5, of which 3 were waited for; matrix products, arithmetic and copies ran while one was open for 0% of the time, Pallas kernels for 11%

profile of v4, /device:TPU:8, one launch (start us, length us, event | category | flops | bytes accessed | tf_op | source)
XLA Modules:
  0.0 39.3 jit_solution(11551507322832596891)
XLA Ops:
  0.6 1.4 %face.1 = (f32[64,128]{1,0:T(8,128)S(1)}, f32[64,128]{1,0:T(8,128)S(1)}, f32[16,128]{1,0:T(8,128)S(1)}, f32[4,64,128]{2,1,0:T(8,128)S(1)}, f32[4,64,128]{2,1,0:T(8,128)S(1)}) custom-call(f32[19,4,16,256]{3,2,1,0:T(8,128)} %pops.3, f32[4,64,128]{2,1,0:T(8,128)} %temp.1, f32[4,64,128]{2,1,0:T(8,128)} %cond.1, f32[4,128]{1,0:T(4,128)} %load.1, f32[4,128]{1,0:T(4,128)} %cool.1), custom_call_target="tpu_custom_call" | custom-call | tf_op jit(solution)/shard_map/face/pallas_call | solution.py:550
  2.1 10.9 %collective-permute-start = (f32[64,128]{1,0:T(8,128)S(1)}, f32[64,128]{1,0:T(8,128)S(1)}, u32[]{:S(2)}, u32[]{:S(2)}) collective-permute-start(f32[64,128]{1,0:T(8,128)S(1)} %get-tuple-element.25.zbuf), channel_id=1, source_target_pairs={{0,1},{1,0},{2,3},{3,2},{4,5},{5,4},{6,7},{7,6},{8,9},{9,8},{10,11... | collective-permute-start | bytes 98312 | tf_op jit(solution)/shard_map/ppermute | solution.py:578
  13.0 1.8 %collide.1 = (f32[19,4,16,256]{3,2,1,0:T(8,128)S(1)}, f32[16,128]{1,0:T(8,128)S(1)}, f32[16,128]{1,0:T(8,128)S(1)}, f32[440,128]{1,0:T(8,128)S(1)}, f32[440,128]...) custom-call(f32[19,4,16,256]{3,2,1,0:T(8,128)} %pops.3, s32[4,256]{1,0:T(4,128)} %nozzle.1, s32[4,256]{1,0:T(4,128)} %wall.1, ...), custom_call_target="tpu_custom_call" | custom-call | tf_op jit(solution)/shard_map/collide/pallas_call | solution.py:550
  14.8 0.1 collective-permute-done.zin
  14.9 1.9 %collective-permute-start.1 = (f32[48,128]{1,0:T(8,128)S(1)}, f32[48,128]{1,0:T(8,128)S(1)}, u32[]{:S(2)}, u32[]{:S(2)}) collective-permute-start(f32[48,128]{1,0:T(8,128)S(1)} %get-tuple-element.32), channel_id=1, source_target_pairs={{0,2},{2,0},{4,6},{6,4},{8,10},{10,8},{12,14},{14,12},{1,3},{3,1},... | collective-permute-start | bytes 73736 | tf_op jit(solution)/shard_map/ppermute | solution.py:587
  16.8 5.3 %collective-permute-start.2 = (f32[48,128]{1,0:T(8,128)S(1)}, f32[48,128]{1,0:T(8,128)S(1)}, u32[]{:S(2)}, u32[]{:S(2)}) collective-permute-start(f32[48,128]{1,0:T(8,128)S(1)} %get-tuple-element.33), channel_id=1, source_target_pairs={{0,14},{2,4},{4,2},{6,8},{8,6},{10,12},{12,10},{14,0},{1,15},{3,5}... | collective-permute-start | bytes 73736 | tf_op jit(solution)/shard_map/ppermute | solution.py:588
  22.1 0.8 %inner.1.pops.whole = f32[19,4,16,256]{3,2,1,0:T(8,128)} custom-call(f32[19,4,16,256]{3,2,1,0:T(8,128)S(1)} %get-tuple-element.24.post, f32[64,128]{1,0:T(8,128)S(1)} %collective-permute-done.zin, s32[4,256]{1,0:T(4,128)S(1)} %get-tuple-element.26.nozzle, s32[4,256]{1,0:T(4,128)S(1)} %get-tuple-element.27.wall), custom_call_target="tpu_custom_call" | custom-call | tf_op jit(solution)/shard_map/inner/pallas_call | solution.py:550
  23.0 0.0 collective-permute-done.1.ya
  23.0 0.8 %collective-permute-done.2.yb = f32[48,128]{1,0:T(8,128)S(1)} collective-permute-done((f32[48,128]{1,0:T(8,128)S(1)}, f32[48,128]{1,0:T(8,128)S(1)}, u32[]{:S(2)}, u32[]{:S(2)}) %collective-permute-start.2) | collective-permute-done | bytes 24608 | tf_op jit(solution)/shard_map/ppermute | solution.py:588
  23.8 0.1 pack_x.1
  23.9 3.5 %collective-permute-start.3 = (f32[440,128]{1,0:T(8,128)S(1)}, f32[440,128]{1,0:T(8,128)S(1)}, u32[]{:S(2)}, u32[]{:S(2)}) collective-permute-start(f32[440,128]{1,0:T(8,128)S(1)} %get-tuple-element.37), channel_id=1, source_target_pairs={{0,496},{1,497},{16,32},{17,33},{32,16},{33,17},{48,64},{49,65},{6... | collective-permute-start | bytes 675848 | tf_op jit(solution)/shard_map/ppermute | solution.py:597
  27.4 6.4 %collective-permute-start.4 = (f32[440,128]{1,0:T(8,128)S(1)}, f32[440,128]{1,0:T(8,128)S(1)}, u32[]{:S(2)}, u32[]{:S(2)}) collective-permute-start(f32[440,128]{1,0:T(8,128)S(1)} %get-tuple-element.38), channel_id=1, source_target_pairs={{0,16},{1,17},{16,0},{17,1},{32,48},{33,49},{48,32},{49,33},{64,80... | collective-permute-start | bytes 675848 | tf_op jit(solution)/shard_map/ppermute | solution.py:598
  33.8 1.0 %side.1.whole = f32[19,4,16,256]{3,2,1,0:T(8,128)} custom-call(f32[19,4,16,256]{3,2,1,0:T(8,128)} %inner.1.pops.whole, f32[19,4,16,256]{3,2,1,0:T(8,128)S(1)} %get-tuple-element.24.post, f32[64,128]{1,0:T(8,128)S(1)} %collective-permute-done.zin, f32[48,128]{1,0:T(8,128)S(1)} %get-tuple-element.35.ypin, ...), custom_call_target="tpu_custom_call", output_to_operand_aliasing={{}: (0, {})} | custom-call | tf_op jit(solution)/shard_map/side/pallas_call | solution.py:550
  34.9 0.7 %sink.1 = (f32[6,4,64,128]{3,2,1,0:T(8,128)S(1)}, f32[2,4,64,128]{3,2,1,0:T(8,128)S(1)}) custom-call(f32[4,64,128]{2,1,0:T(8,128)S(1)} %get-tuple-element.22.tempv.temp, f32[4,64,128]{2,1,0:T(8,128)S(1)} %get-tuple-element.23.condv.cond, f32[64,128]{1,0:T(8,128)S(1)} %get-tuple-element.39.own, f32[16,128]{1,0:T(8,128)S(1)} %get-tuple-element.34.misc, ...), custom_call_target="tpu_custom_call" | custom-call | tf_op jit(solution)/shard_map/sink/pallas_call | solution.py:550
  35.6 0.0 collective-permute-done.3.xa
  35.6 2.3 %collective-permute-done.4.xb = f32[440,128]{1,0:T(8,128)S(1)} collective-permute-done((f32[440,128]{1,0:T(8,128)S(1)}, f32[440,128]{1,0:T(8,128)S(1)}, u32[]{:S(2)}, u32[]{:S(2)}) %collective-permute-start.4) | collective-permute-done | bytes 225312 | tf_op jit(solution)/shard_map/ppermute | solution.py:598
  37.9 1.4 %finish.1 = (f32[19,4,16,256]{3,2,1,0:T(8,128)}, f32[4,64,128]{2,1,0:T(8,128)}) custom-call(f32[19,4,16,256]{3,2,1,0:T(8,128)} %side.1.whole, f32[19,4,16,256]{3,2,1,0:T(8,128)S(1)} %get-tuple-element.24.post, f32[64,128]{1,0:T(8,128)S(1)} %collective-permute-done.zin, f32[48,128]{1,0:T(8,128)S(1)} %get-tuple-element.35.ypin, ...), custom_call_target="tpu_custom_call", output_to_operand_aliasing={{0}: (0, {})} | custom-call | tf_op jit(solution)/shard_map/finish/pallas_call | solution.py:550
  (1 shorter events, 0.0 us)
Async XLA Ops:
  2.1 12.8 %collective-permute-start = (f32[64,128]{1,0:T(8,128)S(1)}, f32[64,128]{1,0:T(8,128)S(1)}, u32[]{:S(2)}, u32[]{:S(2)}) collective-permute-start(f32[64,128]{1,0:T(8,128)S(1)} %get-tuple-element.25.zbuf), channel_id=1, source_target_pairs={{0,1},{1,0},{2,3},{3,2},{4,5},{5,4},{6,7},{7,6},{8,9},{9,8},{10,11... | collective-permute-start | bytes 98312 | tf_op jit(solution)/shard_map/ppermute | solution.py:578
  14.9 8.1 %collective-permute-start.1 = (f32[48,128]{1,0:T(8,128)S(1)}, f32[48,128]{1,0:T(8,128)S(1)}, u32[]{:S(2)}, u32[]{:S(2)}) collective-permute-start(f32[48,128]{1,0:T(8,128)S(1)} %get-tuple-element.32), channel_id=1, source_target_pairs={{0,2},{2,0},{4,6},{6,4},{8,10},{10,8},{12,14},{14,12},{1,3},{3,1},... | collective-permute-start | bytes 73736 | tf_op jit(solution)/shard_map/ppermute | solution.py:587
  16.8 7.0 %collective-permute-start.2 = (f32[48,128]{1,0:T(8,128)S(1)}, f32[48,128]{1,0:T(8,128)S(1)}, u32[]{:S(2)}, u32[]{:S(2)}) collective-permute-start(f32[48,128]{1,0:T(8,128)S(1)} %get-tuple-element.33), channel_id=1, source_target_pairs={{0,14},{2,4},{4,2},{6,8},{8,6},{10,12},{12,10},{14,0},{1,15},{3,5}... | collective-permute-start | bytes 73736 | tf_op jit(solution)/shard_map/ppermute | solution.py:588
  23.9 11.7 %collective-permute-start.3 = (f32[440,128]{1,0:T(8,128)S(1)}, f32[440,128]{1,0:T(8,128)S(1)}, u32[]{:S(2)}, u32[]{:S(2)}) collective-permute-start(f32[440,128]{1,0:T(8,128)S(1)} %get-tuple-element.37), channel_id=1, source_target_pairs={{0,496},{1,497},{16,32},{17,33},{32,16},{33,17},{48,64},{49,65},{6... | collective-permute-start | bytes 675848 | tf_op jit(solution)/shard_map/ppermute | solution.py:597
  27.4 10.5 %collective-permute-start.4 = (f32[440,128]{1,0:T(8,128)S(1)}, f32[440,128]{1,0:T(8,128)S(1)}, u32[]{:S(2)}, u32[]{:S(2)}) collective-permute-start(f32[440,128]{1,0:T(8,128)S(1)} %get-tuple-element.38), channel_id=1, source_target_pairs={{0,16},{1,17},{16,0},{17,1},{32,48},{33,49},{48,32},{49,33},{64,80... | collective-permute-start | bytes 675848 | tf_op jit(solution)/shard_map/ppermute | solution.py:598

commit v5 on v4

--- a/solution.py
+++ b/solution.py
@@ -106,7 +106,7 @@
     return (lax.axis_index("gx") & 1) == jnp.where(odd, 1, 0)
 
 
-def face_kernel(pops, temp, cond, load, cool, zbuf, own, misc, tempv, condv, buf, sems):
+def face_kernel(pops, temp, cond, load, cool, zbuf, own, misc, tempv, condv, popsv, buf, sems):
     low = lax.axis_index("gz") == 0
     face = jnp.where(low, SZ_ - 1, 0)
     fields = [
@@ -128,6 +128,8 @@
     ]
     for copy in rows[0] + fields:
         copy.start()
+    whole = pltpu.make_async_copy(pops, popsv, sems.at[8])
+    whole.start()
 
     @pl.when(low)
     def _():
@@ -174,15 +176,15 @@
     zbuf[Z_E : Z_E + 4, :] = misc[12:16, :]
     zbuf[Z_E + 4 : Z_E + 5, :] = row
     zbuf[Z_E + 5 : Z_E + 8, :] = jnp.zeros((3, HALF), F32)
-
-
-def collide_kernel(pops, nozzle, wall, tempv, condv, post, yp, ym, xa, xb, nozzlev, wallv, buf, face, sems):
-    copies = [pltpu.make_async_copy(pops.at[:, x], buf.at[:, x], sems.at[x]) for x in range(SX)]
+    whole.wait()
+
+
+def collide_kernel(nozzle, wall, buf, tempv, condv, post, yp, ym, xa, xb, nozzlev, wallv, face, sems):
     plates = [
-        pltpu.make_async_copy(nozzle, nozzlev, sems.at[SX]),
-        pltpu.make_async_copy(wall, wallv, sems.at[SX + 1]),
+        pltpu.make_async_copy(nozzle, nozzlev, sems.at[0]),
+        pltpu.make_async_copy(wall, wallv, sems.at[1]),
     ]
-    for copy in copies + plates:
+    for copy in plates:
         copy.start()
     paired = checker()
     for k, field in enumerate((tempv, condv)):
@@ -195,7 +197,6 @@
     y_dn = [jnp.zeros((8, HALF), F32) for _ in range(2)]
     lane8 = lanes((8, HALF))
     for x in range(SX):
-        copies[x].wait()
         for k in range(2):
             z = slice(8 * k, 8 * k + 8)
             for h in range(2):
@@ -569,19 +570,20 @@
 
 def body(populations, nozzle_mask, wall_type, solid_temp, diffusion, heat_load, coolant_temp):
     dma = pltpu.SemaphoreType.DMA
-    zbuf, own, misc, temp, cond = call(
+    zbuf, own, misc, temp, cond, held = call(
         face_kernel, "face",
         far(populations, solid_temp, diffusion, heat_load, coolant_temp),
-        [near(Z_ROWS, HALF), near(DEPTH, HALF), near(16, HALF), near(SX, DEPTH, HALF), near(SX, DEPTH, HALF)],
-        [pltpu.VMEM((2, 19, 8, HALF), F32), dma((8,))],
+        [near(Z_ROWS, HALF), near(DEPTH, HALF), near(16, HALF), near(SX, DEPTH, HALF), near(SX, DEPTH, HALF),
+         near(19, SX, SZ_, 2 * HALF)],
+        [pltpu.VMEM((2, 19, 8, HALF), F32), dma((9,))],
     )
     zin = lax.ppermute(zbuf, "gz", ring("gz", 1))
     post, yp, ym, xa, xb, nozzle, wall = call(
         collide_kernel, "collide",
-        far(populations, nozzle_mask, wall_type) + kept(temp, cond),
+        far(nozzle_mask, wall_type) + kept(held, temp, cond),
         [near(19, SX, SZ_, 2 * HALF), near(16, HALF), near(16, HALF), near(X_ROWS, HALF), near(X_ROWS, HALF),
          pltpu.VMEM((SX, 2 * HALF), jnp.int32), pltpu.VMEM((SX, 2 * HALF), jnp.int32)],
-        [pltpu.VMEM((19, SX, SZ_, 2 * HALF), F32), pltpu.VMEM((X_U, HALF), F32), dma((SX + 2,))],
+        [pltpu.VMEM((X_U, HALF), F32), dma((2,))],
     )
     yao, ybo = call(y_kernel, "pack_y", kept(yp, ym, zbuf, zin), [near(Y_ROWS, HALF)] * 2)
     ya = lax.ppermute(yao, "gy", pairs("gy", 0))

time: 39.5 us -> 39.7 us (level)
  waiting for transfers between devices: 3.18 us -> 3.94 us
  Pallas kernels: 7.35 us -> 6.76 us
    ppermute x1, waiting for transfers between devices: 0.08 us -> 0.84 us  [body(): zin = lax.ppermute(zbuf, 'gz', ring('gz', 1))]
    pallas_call x8, Pallas kernels: 7.35 us -> 6.76 us  [call(): pl.pallas_call(kernel, name=name, in_specs=spaces, out_specs=[ANY if o.me...]
  transfers between devices with their start and end apart: 5 -> 5, of which waited for: 3 -> 3; matrix products, arithmetic and copies ran while one was open for 0% -> 0% of each run, Pallas kernels for 11% -> 9%
where the time goes in v5:
time: 39.7 us; the launch traced here: 39.5 us
  starting transfers between devices  28 us (71%)
  Pallas kernels  6.76 us (17%)
  waiting for transfers between devices  3.94 us (10%)
  between operations  0.73 us (2%)
    ppermute x1, starting transfers between devices, body(): zin = lax.ppermute(zbuf, 'gz', ring('gz', 1))  10.9 us
    pallas_call x8, Pallas kernels, call(): pl.pallas_call(kernel, name=name, in_specs=spaces, out_specs=[ANY if o.me...  6.76 us
    ppermute x1, starting transfers between devices, body(): xb = lax.ppermute(xbo, ('gx', 'gy', 'gz'), checker_pairs(1))  6.45 us
    ppermute x1, starting transfers between devices, body(): yb = lax.ppermute(ybo, 'gy', pairs('gy', 1))  5.27 us
    ppermute x1, starting transfers between devices, body(): xa = lax.ppermute(xao, ('gx', 'gy', 'gz'), checker_pairs(0))  3.47 us
    ppermute x1, waiting for transfers between devices, body(): xb = lax.ppermute(xbo, ('gx', 'gy', 'gz'), checker_pairs(1))  2.28 us
    ppermute x1, starting transfers between devices, body(): ya = lax.ppermute(yao, 'gy', pairs('gy', 0))  1.92 us
    ppermute x1, waiting for transfers between devices, body(): zin = lax.ppermute(zbuf, 'gz', ring('gz', 1))  0.84 us
  transfers between devices with their start and end apart: 5, of which 3 were waited for; matrix products, arithmetic and copies ran while one was open for 0% of the time, Pallas kernels for 9%

profile of v5, /device:TPU:8, one launch (start us, length us, event | category | flops | bytes accessed | tf_op | source)
XLA Modules:
  0.0 39.5 jit_solution(5107057078772209255)
XLA Ops:
  0.6 1.6 %face.1 = (f32[64,128]{1,0:T(8,128)S(1)}, f32[64,128]{1,0:T(8,128)S(1)}, f32[16,128]{1,0:T(8,128)S(1)}, f32[4,64,128]{2,1,0:T(8,128)S(1)}, f32[4,64,128]{2,1,0:T(8,128)S(1)}, /*index=5*/f32[19,4,16,256]{3,2,1,0:T(8,128)S(1)}) custom-call(f32[19,4,16,256]{3,2,1,0:T(8,128)} %pops.1, f32[4,64,128]{2,1,0:T(8,128)} %temp.1, f32[4,64,128]{2,1,0:T(8,128)} %cond.1, ...), custom_call_target="tpu_custom_call" | custom-call | tf_op jit(solution)/shard_map/face/pallas_call | solution.py:551
  2.2 10.9 %collective-permute-start = (f32[64,128]{1,0:T(8,128)S(1)}, f32[64,128]{1,0:T(8,128)S(1)}, u32[]{:S(2)}, u32[]{:S(2)}) collective-permute-start(f32[64,128]{1,0:T(8,128)S(1)} %get-tuple-element.27.zbuf), channel_id=1, source_target_pairs={{0,1},{1,0},{2,3},{3,2},{4,5},{5,4},{6,7},{7,6},{8,9},{9,8},{10,11... | collective-permute-start | bytes 98312 | tf_op jit(solution)/shard_map/ppermute | solution.py:580
  13.2 1.1 %collide.1 = (f32[19,4,16,256]{3,2,1,0:T(8,128)S(1)}, f32[16,128]{1,0:T(8,128)S(1)}, f32[16,128]{1,0:T(8,128)S(1)}, f32[440,128]{1,0:T(8,128)S(1)}, f32[440,128]...) custom-call(s32[4,256]{1,0:T(4,128)} %nozzle.1, s32[4,256]{1,0:T(4,128)} %wall.1, ...), custom_call_target="tpu_custom_call" | custom-call | tf_op jit(solution)/shard_map/collide/pallas_call | solution.py:551
  14.2 0.8 %collective-permute-done.zin = f32[64,128]{1,0:T(8,128)S(1)} collective-permute-done((f32[64,128]{1,0:T(8,128)S(1)}, f32[64,128]{1,0:T(8,128)S(1)}, u32[]{:S(2)}, u32[]{:S(2)}) %collective-permute-start) | collective-permute-done | bytes 32800 | tf_op jit(solution)/shard_map/ppermute | solution.py:580
  15.1 1.9 %collective-permute-start.1 = (f32[48,128]{1,0:T(8,128)S(1)}, f32[48,128]{1,0:T(8,128)S(1)}, u32[]{:S(2)}, u32[]{:S(2)}) collective-permute-start(f32[48,128]{1,0:T(8,128)S(1)} %get-tuple-element.34), channel_id=1, source_target_pairs={{0,2},{2,0},{4,6},{6,4},{8,10},{10,8},{12,14},{14,12},{1,3},{3,1},... | collective-permute-start | bytes 73736 | tf_op jit(solution)/shard_map/ppermute | solution.py:589
  17.0 5.3 %collective-permute-start.2 = (f32[48,128]{1,0:T(8,128)S(1)}, f32[48,128]{1,0:T(8,128)S(1)}, u32[]{:S(2)}, u32[]{:S(2)}) collective-permute-start(f32[48,128]{1,0:T(8,128)S(1)} %get-tuple-element.35), channel_id=1, source_target_pairs={{0,14},{2,4},{4,2},{6,8},{8,6},{10,12},{12,10},{14,0},{1,15},{3,5}... | collective-permute-start | bytes 73736 | tf_op jit(solution)/shard_map/ppermute | solution.py:590
  22.3 0.8 %inner.1.pops.whole = f32[19,4,16,256]{3,2,1,0:T(8,128)} custom-call(f32[19,4,16,256]{3,2,1,0:T(8,128)S(1)} %get-tuple-element.26.post, f32[64,128]{1,0:T(8,128)S(1)} %collective-permute-done.zin, s32[4,256]{1,0:T(4,128)S(1)} %get-tuple-element.28.nozzle, s32[4,256]{1,0:T(4,128)S(1)} %get-tuple-element.29.wall), custom_call_target="tpu_custom_call" | custom-call | tf_op jit(solution)/shard_map/inner/pallas_call | solution.py:551
  23.2 0.0 collective-permute-done.1.ya
  23.2 0.8 %collective-permute-done.2.yb = f32[48,128]{1,0:T(8,128)S(1)} collective-permute-done((f32[48,128]{1,0:T(8,128)S(1)}, f32[48,128]{1,0:T(8,128)S(1)}, u32[]{:S(2)}, u32[]{:S(2)}) %collective-permute-start.2) | collective-permute-done | bytes 24608 | tf_op jit(solution)/shard_map/ppermute | solution.py:590
  24.0 0.1 pack_x.1
  24.1 3.5 %collective-permute-start.3 = (f32[440,128]{1,0:T(8,128)S(1)}, f32[440,128]{1,0:T(8,128)S(1)}, u32[]{:S(2)}, u32[]{:S(2)}) collective-permute-start(f32[440,128]{1,0:T(8,128)S(1)} %get-tuple-element.39), channel_id=1, source_target_pairs={{0,496},{1,497},{16,32},{17,33},{32,16},{33,17},{48,64},{49,65},{6... | collective-permute-start | bytes 675848 | tf_op jit(solution)/shard_map/ppermute | solution.py:599
  27.6 6.4 %collective-permute-start.4 = (f32[440,128]{1,0:T(8,128)S(1)}, f32[440,128]{1,0:T(8,128)S(1)}, u32[]{:S(2)}, u32[]{:S(2)}) collective-permute-start(f32[440,128]{1,0:T(8,128)S(1)} %get-tuple-element.40), channel_id=1, source_target_pairs={{0,16},{1,17},{16,0},{17,1},{32,48},{33,49},{48,32},{49,33},{64,80... | collective-permute-start | bytes 675848 | tf_op jit(solution)/shard_map/ppermute | solution.py:600
  34.0 1.0 %side.1.whole = f32[19,4,16,256]{3,2,1,0:T(8,128)} custom-call(f32[19,4,16,256]{3,2,1,0:T(8,128)} %inner.1.pops.whole, f32[19,4,16,256]{3,2,1,0:T(8,128)S(1)} %get-tuple-element.26.post, f32[64,128]{1,0:T(8,128)S(1)} %collective-permute-done.zin, f32[48,128]{1,0:T(8,128)S(1)} %get-tuple-element.37.ypin, ...), custom_call_target="tpu_custom_call", output_to_operand_aliasing={{}: (0, {})} | custom-call | tf_op jit(solution)/shard_map/side/pallas_call | solution.py:551
  35.1 0.7 %sink.1 = (f32[6,4,64,128]{3,2,1,0:T(8,128)S(1)}, f32[2,4,64,128]{3,2,1,0:T(8,128)S(1)}) custom-call(f32[4,64,128]{2,1,0:T(8,128)S(1)} %get-tuple-element.24.tempv.temp, f32[4,64,128]{2,1,0:T(8,128)S(1)} %get-tuple-element.25.condv.cond, f32[64,128]{1,0:T(8,128)S(1)} %get-tuple-element.41.own, f32[16,128]{1,0:T(8,128)S(1)} %get-tuple-element.36.misc, ...), custom_call_target="tpu_custom_call" | custom-call | tf_op jit(solution)/shard_map/sink/pallas_call | solution.py:551
  35.8 0.0 collective-permute-done.3.xa
  35.8 2.3 %collective-permute-done.4.xb = f32[440,128]{1,0:T(8,128)S(1)} collective-permute-done((f32[440,128]{1,0:T(8,128)S(1)}, f32[440,128]{1,0:T(8,128)S(1)}, u32[]{:S(2)}, u32[]{:S(2)}) %collective-permute-start.4) | collective-permute-done | bytes 225312 | tf_op jit(solution)/shard_map/ppermute | solution.py:600
  38.1 1.4 %finish.1 = (f32[19,4,16,256]{3,2,1,0:T(8,128)}, f32[4,64,128]{2,1,0:T(8,128)}) custom-call(f32[19,4,16,256]{3,2,1,0:T(8,128)} %side.1.whole, f32[19,4,16,256]{3,2,1,0:T(8,128)S(1)} %get-tuple-element.26.post, f32[64,128]{1,0:T(8,128)S(1)} %collective-permute-done.zin, f32[48,128]{1,0:T(8,128)S(1)} %get-tuple-element.37.ypin, ...), custom_call_target="tpu_custom_call", output_to_operand_aliasing={{0}: (0, {})} | custom-call | tf_op jit(solution)/shard_map/finish/pallas_call | solution.py:551
  (1 shorter events, 0.0 us)
Async XLA Ops:
  2.2 12.8 %collective-permute-start = (f32[64,128]{1,0:T(8,128)S(1)}, f32[64,128]{1,0:T(8,128)S(1)}, u32[]{:S(2)}, u32[]{:S(2)}) collective-permute-start(f32[64,128]{1,0:T(8,128)S(1)} %get-tuple-element.27.zbuf), channel_id=1, source_target_pairs={{0,1},{1,0},{2,3},{3,2},{4,5},{5,4},{6,7},{7,6},{8,9},{9,8},{10,11... | collective-permute-start | bytes 98312 | tf_op jit(solution)/shard_map/ppermute | solution.py:580
  15.1 8.1 %collective-permute-start.1 = (f32[48,128]{1,0:T(8,128)S(1)}, f32[48,128]{1,0:T(8,128)S(1)}, u32[]{:S(2)}, u32[]{:S(2)}) collective-permute-start(f32[48,128]{1,0:T(8,128)S(1)} %get-tuple-element.34), channel_id=1, source_target_pairs={{0,2},{2,0},{4,6},{6,4},{8,10},{10,8},{12,14},{14,12},{1,3},{3,1},... | collective-permute-start | bytes 73736 | tf_op jit(solution)/shard_map/ppermute | solution.py:589
  17.0 7.0 %collective-permute-start.2 = (f32[48,128]{1,0:T(8,128)S(1)}, f32[48,128]{1,0:T(8,128)S(1)}, u32[]{:S(2)}, u32[]{:S(2)}) collective-permute-start(f32[48,128]{1,0:T(8,128)S(1)} %get-tuple-element.35), channel_id=1, source_target_pairs={{0,14},{2,4},{4,2},{6,8},{8,6},{10,12},{12,10},{14,0},{1,15},{3,5}... | collective-permute-start | bytes 73736 | tf_op jit(solution)/shard_map/ppermute | solution.py:590
  24.1 11.7 %collective-permute-start.3 = (f32[440,128]{1,0:T(8,128)S(1)}, f32[440,128]{1,0:T(8,128)S(1)}, u32[]{:S(2)}, u32[]{:S(2)}) collective-permute-start(f32[440,128]{1,0:T(8,128)S(1)} %get-tuple-element.39), channel_id=1, source_target_pairs={{0,496},{1,497},{16,32},{17,33},{32,16},{33,17},{48,64},{49,65},{6... | collective-permute-start | bytes 675848 | tf_op jit(solution)/shard_map/ppermute | solution.py:599
  27.6 10.5 %collective-permute-start.4 = (f32[440,128]{1,0:T(8,128)S(1)}, f32[440,128]{1,0:T(8,128)S(1)}, u32[]{:S(2)}, u32[]{:S(2)}) collective-permute-start(f32[440,128]{1,0:T(8,128)S(1)} %get-tuple-element.40), channel_id=1, source_target_pairs={{0,16},{1,17},{16,0},{17,1},{32,48},{33,49},{48,32},{49,33},{64,80... | collective-permute-start | bytes 675848 | tf_op jit(solution)/shard_map/ppermute | solution.py:600
